TPU v7x, 128 devices: a whole 4x4x4 slice. The times are simulated.
128 devices in a mesh: band: 8 (over y, z_hi), plane: 16 (over z_lo, x, core).
Axes of the slice: x: 4, y: 4, z: 4 (z_hi: 2, z_lo: 2; z = z_hi * 2 + z_lo), core: 2. Of those that a mesh axis runs over, the one named last changes fastest.
Arguments:
- orbitals: float32 [64, 96, 9216], P('band', 'plane'), may hold values from -6 to 6
Outputs:
- exchange_action: float32 [64, 96, 9216], P('band', 'plane')
All inputs are finite; a program needn't handle non-finite values.
Results may differ from a plain program's by a relative error of at most 0.0001.
Values sent between devices are 32-bit elements; how exact they have to be, the bound alone decides.
A program may use at most 128 MiB of HBM per device.

v0:
```python
import math

import jax
import jax.numpy as jnp
from jax import lax
from jax.sharding import PartitionSpec as P

PAIR = 2
ROUNDS = 4


OMEGA = 0.106
CELL = 41.05
ALPHA = 0.25
HIGHEST = lax.Precision.HIGHEST


def from_root(value, axis, source):
    kept = jnp.where(lax.axis_index(axis) == source, value, 0).astype(value.dtype)
    return lax.psum(kept, axis)


def hartley_table(count):
    index = jnp.arange(count, dtype=jnp.int32)
    product = index[:, None] * index[None, :] % count
    angle = product.astype(jnp.float32) * (2.0 * math.pi / count)
    return jnp.cos(angle) + jnp.sin(angle)


def frequencies(count):
    index = jnp.arange(count, dtype=jnp.int32)
    return jnp.where(index <= count // 2, index, index - count).astype(jnp.float32)


def screened_kernel(count, first, width):
    freq = frequencies(count)
    square = freq * freq
    middle = lax.dynamic_slice_in_dim(square, first, width)
    scale = (2.0 * math.pi / CELL) ** 2
    g_two = scale * (square[:, None, None] + middle[None, :, None] + square[None, None, :])
    positive = g_two > 0
    safe = jnp.where(positive, g_two, 1.0)
    value = 4.0 * math.pi / safe * -jnp.expm1(-safe / (4.0 * OMEGA * OMEGA))
    value = jnp.where(positive, value, math.pi / (OMEGA * OMEGA))
    return value / float(count**3)


def coulomb_solve(density, table, kernel):
    field = jnp.einsum("pxyz,zw->pxyw", density, table, precision=HIGHEST)
    field = jnp.einsum("pxyz,yv->pxvz", field, table, precision=HIGHEST)
    field = lax.all_to_all(field, "plane", split_axis=2, concat_axis=1, tiled=True)
    field = jnp.einsum("pxyz,xu->puyz", field, table, precision=HIGHEST) * kernel
    field = jnp.einsum("pxyz,xu->puyz", field, table, precision=HIGHEST)
    field = lax.all_to_all(field, "plane", split_axis=1, concat_axis=2, tiled=True)
    field = jnp.einsum("pxyz,zw->pxyw", field, table, precision=HIGHEST)
    return jnp.einsum("pxyz,yv->pxvz", field, table, precision=HIGHEST)


def fetch_pair(fields, turn):
    return from_root(fields[0:PAIR], "band", turn)


def local(orbitals):
    local_bands, planes, flat = orbitals.shape
    count = planes * lax.axis_size("plane")
    fields = orbitals.reshape(local_bands, planes, count, count)
    table = hartley_table(count)
    kernel = screened_kernel(count, lax.axis_index("plane") * planes, planes)
    shape_tail = (planes, count, count)
    local_sum = jnp.zeros_like(fields)
    owner_list = []
    for turn in range(ROUNDS):
        received = fetch_pair(fields, turn)
        density = (fields[:, None] * received[None]).reshape((local_bands * PAIR,) + shape_tail)
        potential = coulomb_solve(density, table, kernel).reshape((local_bands, PAIR) + shape_tail)
        local_sum = local_sum + jnp.sum(received[None] * potential, axis=1)
        owner_list.append(jnp.sum(fields[:, None] * potential, axis=0))
    owner_terms = jnp.stack(owner_list)
    own_extra = jnp.zeros((PAIR,) + shape_tail, jnp.float32)
    for turn in range(ROUNDS):
        summed = lax.psum(owner_terms[turn], "band")
        owner_flag = (lax.axis_index("band") == turn).astype(jnp.float32)
        own_extra = own_extra + owner_flag * summed
    local_sum = local_sum.at[0:PAIR].add(own_extra)
    return (-ALPHA * local_sum).reshape(local_bands, planes, count * count)


def solution(mesh):
    placed = (P("band", "plane", None),)
    return jax.shard_map(
        local, mesh=mesh, in_specs=placed, out_specs=P("band", "plane", None), check_vma=False
    )
```

profile of v0, /device:TPU:8, one launch (start us, length us, event | category | flops | bytes accessed | tf_op | source)
XLA Modules:
  0.0 886.8 jit_solution(3193934926200104955)
XLA Ops:
  13.7 2.4 mul.424
  16.1 122.7 %all-reduce.7.cloned.1.call-done = (f32[2,6,96,96]{3,2,0,1:T(8,128)}, f32[2,6,96,96]{3,2,0,1:T(8,128)}, f32[2,6,96,96]{3,2,0,1:T(8,128)}, f32[2,6,96,96]{3,2,0,1:T(8,128)}) async-done(((f32[2,6,96,96]{3,2,0,1:T(8,128)}, f32[2,6,96,96]{3,2,0,1:T(8,128)}, f32[2,6,96,96]{3,2,0,1:T(8,128)}, f32[2,6,96,96]{3,2,0,1:T(8,128)}), (f32[2,6,96,96]{3,2,0,1:T(8,128)}, f32[2,6,96,96]{3,2,0,1:T(8,128)}, ...) | async-done | bytes 1769488 | tf_op jit(solution)/shard_map/psum | solution.py:20
  138.8 9.3 %broadcast_multiply_fusion.2 = (f32[8,2,6,96,96]{4,3,2,1,0:T(8,128)}, f32[8,2,6,96,96]{4,3,2,1,0:T(8,128)}, f32[8,2,6,96,96]{4,3,2,1,0:T(8,128)}, f32[8,2,6,96,96]{4,3,2,1,0:T(8,128)}) fusion(f32[2,6,96,96]{3,2,0,1:T(8,128)} %get-tuple-element.27, f32[2,6,96,96]{3,2,0,1:T(8,128)} %get-tuple-element.26, f32[8,6,96,96]{3,2,0,1:T(8,128)S(1)} %mul.424, ...), kind=kLoop, calls=%fused_computation.39 | loop fusion | flops 3538944 | bytes 17694720 | tf_op jit(solution)/shard_map/mul | solution.py:74
  148.1 6.3 fusion.52
  154.4 4.5 convolution_bitcast_fusion.1
  158.9 4.9 copy.143
  163.8 4.8 all-to-all-start.4
  168.6 6.3 fusion.55
  175.0 4.5 convolution_bitcast_fusion.2
  179.5 4.9 copy.133
  184.4 47.5 %all-to-all-done.4 = f32[16,6,96,96]{3,0,1,2:T(8,128)} async-done(((f32[16,6,96,96]{3,0,1,2:T(8,128)}), f32[16,6,96,96]{3,0,1,2:T(8,128)}, u32[]{:S(2)}, u32[]{:S(2)}) %all-to-all-start.4) | async-done | bytes 3538976 | tf_op jit(solution)/shard_map/all_to_all | solution.py:51
  231.9 5.1 all-to-all-start.2
  237.1 6.3 fusion.49
  243.4 4.5 convolution_bitcast_fusion
  247.9 4.9 copy.153
  252.9 47.7 %all-to-all-done.2 = f32[16,6,96,96]{3,0,1,2:T(8,128)} async-done(((f32[16,6,96,96]{3,0,1,2:T(8,128)}), f32[16,6,96,96]{3,0,1,2:T(8,128)}, u32[]{:S(2)}, u32[]{:S(2)}) %all-to-all-start.2) | async-done | bytes 3538976 | tf_op jit(solution)/shard_map/all_to_all | solution.py:51
  300.6 4.7 all-to-all-start.6
  305.3 6.3 fusion.58
  311.7 4.5 convolution_bitcast_fusion.3
  316.2 4.9 copy.123
  321.1 47.7 %all-to-all-done.6 = f32[16,6,96,96]{3,0,1,2:T(8,128)} async-done(((f32[16,6,96,96]{3,0,1,2:T(8,128)}), f32[16,6,96,96]{3,0,1,2:T(8,128)}, u32[]{:S(2)}, u32[]{:S(2)}) %all-to-all-start.6) | async-done | bytes 3538976 | tf_op jit(solution)/shard_map/all_to_all | solution.py:51
  368.8 5.0 all-to-all-start
  374.2 2.9 copy.145
  377.1 7.1 fusion.14
  384.2 4.7 fusion.38
  389.0 4.9 copy.147
  393.9 42.9 %all-to-all-done = f32[16,6,96,96]{3,0,1,2:T(8,128)} async-done(((f32[16,6,96,96]{3,0,1,2:T(8,128)}), f32[16,6,96,96]{3,0,1,2:T(8,128)}, u32[]{:S(2)}, u32[]{:S(2)}) %all-to-all-start) | async-done | bytes 3538976 | tf_op jit(solution)/shard_map/all_to_all | solution.py:51
  436.8 4.6 all-to-all-start.5
  441.4 2.9 copy.135
  444.3 7.1 fusion.18
  451.5 5.0 fusion.35
  456.4 4.9 copy.137
  461.4 43.5 %all-to-all-done.5 = f32[16,96,6,96]{3,0,2,1:T(8,128)} async-done(((f32[16,96,6,96]{3,0,2,1:T(8,128)}), f32[16,96,6,96]{3,0,2,1:T(8,128)}, u32[]{:S(2)}, u32[]{:S(2)}) %all-to-all-start.5) | async-done | bytes 3538976 | tf_op jit(solution)/shard_map/all_to_all | solution.py:54
  504.9 4.6 all-to-all-start.3
  509.5 2.9 copy.155
  512.4 7.1 fusion.10
  519.5 4.7 fusion.41
  524.3 4.9 copy.157
  529.1 43.8 %all-to-all-done.3 = f32[16,96,6,96]{3,0,2,1:T(8,128)} async-done(((f32[16,96,6,96]{3,0,2,1:T(8,128)}), f32[16,96,6,96]{3,0,2,1:T(8,128)}, u32[]{:S(2)}, u32[]{:S(2)}) %all-to-all-start.3) | async-done | bytes 3538976 | tf_op jit(solution)/shard_map/all_to_all | solution.py:54
  572.9 4.6 all-to-all-start.7
  577.5 2.9 copy.125
  580.4 7.4 fusion.22
  587.8 5.3 fusion.32
  593.2 5.0 copy.127
  598.1 42.9 %all-to-all-done.7 = f32[16,96,6,96]{3,0,2,1:T(8,128)} async-done(((f32[16,96,6,96]{3,0,2,1:T(8,128)}), f32[16,96,6,96]{3,0,2,1:T(8,128)}, u32[]{:S(2)}, u32[]{:S(2)}) %all-to-all-start.7) | async-done | bytes 3538976 | tf_op jit(solution)/shard_map/all_to_all | solution.py:54
  641.1 4.6 all-to-all-start.1
  650.4 2.8 copy.148
  653.2 2.8 copy.138
  656.0 2.8 copy.158
  658.8 7.0 fusion.12
  665.7 7.0 fusion.16
  672.7 7.0 fusion.8
  679.8 29.3 %all-to-all-done.1 = f32[16,96,6,96]{3,0,2,1:T(8,128)} async-done(((f32[16,96,6,96]{3,0,2,1:T(8,128)}), f32[16,96,6,96]{3,0,2,1:T(8,128)}, u32[]{:S(2)}, u32[]{:S(2)}) %all-to-all-start.1) | async-done | bytes 3538976 | tf_op jit(solution)/shard_map/all_to_all | solution.py:54
  709.1 2.8 copy.128
  711.9 5.4 fusion.20
  717.4 6.3 multiply_reduce_fusion.6
  723.7 6.6 multiply_reduce_fusion.5
  730.3 6.6 multiply_reduce_fusion.4
  736.9 6.8 multiply_reduce_fusion.7
  743.6 5.3 multiply_reduce_fusion.3
  748.9 4.8 add_add_fusion
  753.7 117.3 %all-reduce.5.cloned.1.call-done = (f32[2,6,96,96]{3,2,1,0:T(8,128)}, f32[2,6,96,96]{3,2,1,0:T(8,128)}, f32[2,6,96,96]{3,2,1,0:T(8,128)}, f32[2,6,96,96]{3,2,1,0:T(8,128)}) async-done(((f32[2,6,96,96]{3,2,1,0:T(8,128)}, f32[2,6,96,96]{3,2,1,0:T(8,128)}, f32[2,6,96,96]{3,2,1,0:T(8,128)}, f32[2,6,96,96]{3,2,1,0:T(8,128)}), (f32[2,6,96,96]{3,2,1,0:T(8,128)}, f32[2,6,96,96]{3,2,1,0:T(8,128)}, ...) | async-done | bytes 1769488 | tf_op jit(solution)/shard_map/psum | solution.py:81
  874.7 2.7 reshape.164
  877.4 2.2 copy.183
  (44 shorter events, 16.0 us)
Async XLA Ops:
  6.5 132.2 %all-reduce.7.cloned.1.call-start = ((), (), s32[]{:S(2)}) async-start(), calls=%async_computation.9 | async-start | bytes 4718592 | tf_op jit(solution)/shard_map/psum | solution.py:20
  163.8 68.1 %all-to-all-start.4 = ((f32[16,6,96,96]{3,0,1,2:T(8,128)}), f32[16,6,96,96]{3,0,1,2:T(8,128)}, u32[]{:S(2)}, u32[]{:S(2)}) async-start(f32[16,6,96,96]{3,0,1,2:T(8,128)} %copy.143), calls=%async_computation.4 | async-start | bytes 9437184 | tf_op jit(solution)/shard_map/all_to_all | solution.py:51
  231.9 68.6 %all-to-all-start.2 = ((f32[16,6,96,96]{3,0,1,2:T(8,128)}), f32[16,6,96,96]{3,0,1,2:T(8,128)}, u32[]{:S(2)}, u32[]{:S(2)}) async-start(f32[16,6,96,96]{3,0,1,2:T(8,128)} %copy.133), calls=%async_computation.2 | async-start | bytes 9437184 | tf_op jit(solution)/shard_map/all_to_all | solution.py:51
  300.6 68.2 %all-to-all-start.6 = ((f32[16,6,96,96]{3,0,1,2:T(8,128)}), f32[16,6,96,96]{3,0,1,2:T(8,128)}, u32[]{:S(2)}, u32[]{:S(2)}) async-start(f32[16,6,96,96]{3,0,1,2:T(8,128)} %copy.153), calls=%async_computation.6 | async-start | bytes 9437184 | tf_op jit(solution)/shard_map/all_to_all | solution.py:51
  368.8 68.1 %all-to-all-start = ((f32[16,6,96,96]{3,0,1,2:T(8,128)}), f32[16,6,96,96]{3,0,1,2:T(8,128)}, u32[]{:S(2)}, u32[]{:S(2)}) async-start(f32[16,6,96,96]{3,0,1,2:T(8,128)} %copy.123), calls=%async_computation | async-start | bytes 9437184 | tf_op jit(solution)/shard_map/all_to_all | solution.py:51
  436.8 68.0 %all-to-all-start.5 = ((f32[16,96,6,96]{3,0,2,1:T(8,128)}), f32[16,96,6,96]{3,0,2,1:T(8,128)}, u32[]{:S(2)}, u32[]{:S(2)}) async-start(f32[16,96,6,96]{3,0,2,1:T(8,128)} %copy.147), calls=%async_computation.5 | async-start | bytes 9437184 | tf_op jit(solution)/shard_map/all_to_all | solution.py:54
  504.9 68.0 %all-to-all-start.3 = ((f32[16,96,6,96]{3,0,2,1:T(8,128)}), f32[16,96,6,96]{3,0,2,1:T(8,128)}, u32[]{:S(2)}, u32[]{:S(2)}) async-start(f32[16,96,6,96]{3,0,2,1:T(8,128)} %copy.137), calls=%async_computation.3 | async-start | bytes 9437184 | tf_op jit(solution)/shard_map/all_to_all | solution.py:54
  572.9 68.1 %all-to-all-start.7 = ((f32[16,96,6,96]{3,0,2,1:T(8,128)}), f32[16,96,6,96]{3,0,2,1:T(8,128)}, u32[]{:S(2)}, u32[]{:S(2)}) async-start(f32[16,96,6,96]{3,0,2,1:T(8,128)} %copy.157), calls=%async_computation.7 | async-start | bytes 9437184 | tf_op jit(solution)/shard_map/all_to_all | solution.py:54
  598.1 51.4 %copy-start.1 = (f32[2,6,96,96]{3,2,0,1:T(8,128)S(1)}, f32[2,6,96,96]{3,2,0,1:T(8,128)}, u32[]{:S(2)}) copy-start(f32[2,6,96,96]{3,2,0,1:T(8,128)} %get-tuple-element.27) | copy-start | bytes 1327108
  598.1 52.2 %copy-start = (f32[2,6,96,96]{3,2,0,1:T(8,128)S(1)}, f32[2,6,96,96]{3,2,0,1:T(8,128)}, u32[]{:S(2)}) copy-start(f32[2,6,96,96]{3,2,0,1:T(8,128)} %get-tuple-element.28) | copy-start | bytes 1327108
  641.1 68.0 %all-to-all-start.1 = ((f32[16,96,6,96]{3,0,2,1:T(8,128)}), f32[16,96,6,96]{3,0,2,1:T(8,128)}, u32[]{:S(2)}, u32[]{:S(2)}) async-start(f32[16,96,6,96]{3,0,2,1:T(8,128)} %copy.127), calls=%async_computation.1 | async-start | bytes 9437184 | tf_op jit(solution)/shard_map/all_to_all | solution.py:54
  645.6 225.4 %all-reduce.5.cloned.1.call-start = ((), (), s32[]{:S(2)}) async-start(), calls=%async_computation.8 | async-start | bytes 4718592 | tf_op jit(solution)/shard_map/psum | solution.py:81
  709.1 8.3 slice-start.4
  711.9 5.4 slice-start.5
  711.9 11.8 %slice-start.2 = ((s8[4718592]{0:T(1024)(128)(4,1)}), s8[4194304]{0:T(1024)(128)(4,1)S(1)}, s32[]{:S(2)}) async-start(s8[4718592]{0:T(1024)(128)(4,1)} %bitcast.181), calls=%async_computation.12 | async-start | bytes 8388608
  717.3 6.3 slice-start.3
  717.4 6.3 copy-start.4
  717.4 12.9 %slice-start = ((s8[4718592]{0:T(1024)(128)(4,1)}), s8[4194304]{0:T(1024)(128)(4,1)S(1)}, s32[]{:S(2)}) async-start(s8[4718592]{0:T(1024)(128)(4,1)} %bitcast.179), calls=%async_computation.10 | async-start | bytes 8388608
  723.7 6.6 slice-start.1
  723.7 6.6 copy-start.3
  730.3 6.6 copy-start.2
Sparse Core Ops, SparseCore 0:
  13.8 124.9 all-reduce.6
  749.0 121.9 all-reduce.4
where the time goes:
time: 890 us; the launch traced here: 887 us
  waiting for transfers between devices  585 us (66%)
  matrix products  144 us (16%)
  local copies, waits for them, and re-layouts  79.6 us (9%)
  starting transfers between devices  37.9 us (4%)
  other arithmetic  25.4 us (3%)
  between operations  14.1 us (2%)
    all_to_all x4, waiting for transfers between devices, coulomb_solve(): lax.all_to_all(field, 'plane', split_axis=2, concat_axis=1, tiled=True)  186 us
    all_to_all x4, waiting for transfers between devices, coulomb_solve(): lax.all_to_all(field, 'plane', split_axis=1, concat_axis=2, tiled=True)  160 us
    psum x1, waiting for transfers between devices, from_root(): return lax.psum(kept, axis)  123 us
    psum x1, waiting for transfers between devices, local(): summed = lax.psum(owner_terms[turn], 'band')  117 us
    dot_general x4, matrix products, coulomb_solve(): jnp.einsum('pxyz,xu->puyz', field, table, precision=HIGHEST) * kernel  28.7 us
    dot_general x4, matrix products, coulomb_solve(): field = jnp.einsum('pxyz,zw->pxyw', field, table, precision=HIGHEST)  26.4 us
    dot_general x4, matrix products, coulomb_solve(): return jnp.einsum('pxyz,yv->pxvz', field, table, precision=HIGHEST)  26.2 us
    dot_general x4, matrix products, coulomb_solve(): field = jnp.einsum('pxyz,zw->pxyw', density, table, precision=HIGHEST)  25.4 us
  transfers between devices with their start and end apart: 10, of which 10 were waited for; matrix products, arithmetic and copies ran while one was open for 19% of the time, Pallas kernels for 0%

commit v1 on v0

v1 whole, which is shorter than its diff:
```python
import math, functools
import numpy as np
import jax, jax.numpy as jnp
from jax import lax
from jax.experimental import pallas as pl
from jax.experimental.pallas import tpu as pltpu
from jax.sharding import PartitionSpec as P
import ml_dtypes

N = 96
OMEGA = 0.106
CELL = 41.05
bf = jnp.bfloat16

def split_np(t):
    t = t.astype(np.float32)
    hi = t.astype(ml_dtypes.bfloat16)
    lo = (t - hi.astype(np.float32)).astype(ml_dtypes.bfloat16)
    return hi, lo

def tables():
    k = np.arange(N)
    ang = 2*np.pi*((k[:,None]*k[None,:])%N)/N
    T = np.cos(ang)+np.sin(ang)
    hi, lo = split_np(T)
    wz = np.zeros((4,256,256), ml_dtypes.bfloat16)
    wi = np.zeros((4,256,256), ml_dtypes.bfloat16)
    for l in range(4):
        lane = (96*l + np.arange(N)) % 128
        wz[l, lane, 0:96] = hi
        wz[l, lane, 128:224] = lo
        wz[l, 128+lane, 0:96] = hi
        wi[l, 0:96, lane] = hi.T
        wi[l, 0:96, 128+lane] = lo.T
        wi[l, 128:224, lane] = hi.T
    def two(hi, lo):
        t = np.zeros((192,192), ml_dtypes.bfloat16)
        t[:96,:96]=hi; t[:96,96:]=hi; t[96:,:96]=lo
        return t
    order = np.array([4*kk+l for l in range(4) for kk in range(24)])
    ty = two(hi[:,order], lo[:,order])
    tyi = two(hi[order,:], lo[order,:])
    tx = two(hi, lo)
    return wz, wi, ty, tyi, tx

def kernel_table():
    idx = jnp.arange(N, dtype=jnp.int32)
    f = jnp.where(idx <= N//2, idx, idx-N).astype(jnp.float32)
    sq = f*f
    sqw = jnp.pad(sq, (0,32))
    g2 = (2.0*math.pi/CELL)**2 * (sq[:,None,None]+sq[None,:,None]+sqw[None,None,:])
    pos = g2 > 0
    safe = jnp.where(pos, g2, 1.0)
    val = 4.0*math.pi/safe * -jnp.expm1(-safe/(4.0*OMEGA*OMEGA))
    val = jnp.where(pos, val, math.pi/(OMEGA*OMEGA))
    return (val * (-0.25/float(N**3))).reshape(N*N, 128)

def split(x):
    hi = x.astype(bf)
    lo = (x - hi.astype(jnp.float32)).astype(bf)
    return hi, lo

def dot(a, b):
    return lax.dot_general(a, b, (((1,),(0,)),((),())), preferred_element_type=jnp.float32)

def left(t, x):
    hi, lo = split(x)
    q = dot(t, jnp.concatenate([hi, lo], axis=0))
    return q[:96] + q[96:]

def right(x, w):
    hi, lo = split(x)
    o = dot(jnp.concatenate([hi, lo], axis=1), w)
    return o[:, :128] + o[:, 128:]

def pair(i_ref, j_ref, near_ref, far_ref, a_ref, k_ref, wz_ref, wi_ref, ty_ref, tyi_ref, tx_ref, near_first, far_first, XB=8, VB=4, AS=96, stages=7):
    lane = lax.broadcasted_iota(jnp.int32, (24*XB, 128), 1)
    def fwd(xb, _):
        base = xb*(XB*72)
        d = []
        for s in range(3):
            rows = pl.ds(base+s, 24*XB, stride=3)
            d.append(i_ref[rows, :]*j_ref[rows, :])
        m = [d[0], jnp.where(lane >= 96, d[0], d[1]), jnp.where(lane >= 64, d[1], d[2]), d[2]]
        o = [right(m[l], wz_ref[l]) for l in range(4)]
        for xx in range(0, XB, 2):
            cols = []
            for x in (xx, xx+1):
                cols.append(jnp.concatenate([o[l][24*x:24*x+24] for l in range(4)], axis=0))
            q = left(ty_ref[...], jnp.concatenate(cols, axis=1))
            row = (xb*XB+xx)*AS
            a_ref[pl.ds(row, 96), :] = q[:, :128]
            a_ref[pl.ds(row+AS, 96), :] = q[:, 128:]
        return 0
    if stages & 1:
        lax.fori_loop(0, 96//XB, fwd, 0)
    def mid(vb, _):
        for vv in range(0, VB, 2):
            v = vb*VB+vv
            a = jnp.concatenate([a_ref[pl.ds(v, 96, stride=AS), :], a_ref[pl.ds(v+1, 96, stride=AS), :]], axis=1)
            kk = jnp.concatenate([k_ref[pl.ds(v*96, 96), :], k_ref[pl.ds(v*96+96, 96), :]], axis=1)
            b = left(tx_ref[...], left(tx_ref[...], a) * kk)
            a_ref[pl.ds(v, 96, stride=AS), :] = b[:, :128]
            a_ref[pl.ds(v+1, 96, stride=AS), :] = b[:, 128:]
        return 0
    if stages & 2:
        lax.fori_loop(0, 96//VB, mid, 0)
    def inv(xb, _):
        parts = [[] for _ in range(4)]
        for xx in range(0, XB, 2):
            row = (xb*XB+xx)*AS
            a = jnp.concatenate([a_ref[pl.ds(row, 96), :], a_ref[pl.ds(row+AS, 96), :]], axis=1)
            q = left(tyi_ref[...], a)
            for x in range(2):
                for l in range(4):
                    parts[l].append(q[24*l:24*l+24, 128*x:128*x+128])
        o = [right(jnp.concatenate(parts[l], axis=0), wi_ref[l]) for l in range(4)]
        vs = [jnp.where(lane < 96, o[0], o[1]), jnp.where(lane < 64, o[1], o[2]), jnp.where(lane < 32, o[2], o[3])]
        base = xb*(XB*72)
        for s in range(3):
            rows = pl.ds(base+s, 24*XB, stride=3)
            n = j_ref[rows, :]*vs[s]
            f = i_ref[rows, :]*vs[s]
            near_ref[rows, :] = n if near_first else near_ref[rows, :]+n
            far_ref[rows, :] = f if far_first else far_ref[rows, :]+f
        return 0
    if stages & 4:
        lax.fori_loop(0, 96//XB, inv, 0)


def exchange(i_hbm, j_hbm, k_ref, wz_ref, wi_ref, ty_ref, tyi_ref, tx_ref, near, far, iv, jv, nv, fv, a, sem):
    for g in range(2):
        pltpu.make_async_copy(i_hbm.at[g], iv.at[g], sem.at[g]).start()
        pltpu.make_async_copy(j_hbm.at[g], jv.at[g], sem.at[2 + g]).start()
    for g in range(2):
        pltpu.make_async_copy(i_hbm.at[g], iv.at[g], sem.at[g]).wait()
        pltpu.make_async_copy(j_hbm.at[g], jv.at[g], sem.at[2 + g]).wait()
    for gi, gj in ((0, 0), (0, 1), (1, 1), (1, 0)):
        pair(iv.at[gi], jv.at[gj], nv.at[gi], fv.at[gj], a, k_ref, wz_ref, wi_ref, ty_ref, tyi_ref, tx_ref,
             gj == gi, gi == 0, AS=97)
    for g in range(2):
        pltpu.make_async_copy(nv.at[g], near.at[g], sem.at[g]).start()
        pltpu.make_async_copy(fv.at[g], far.at[g], sem.at[2 + g]).start()
    for g in range(2):
        pltpu.make_async_copy(nv.at[g], near.at[g], sem.at[g]).wait()
        pltpu.make_async_copy(fv.at[g], far.at[g], sem.at[2 + g]).wait()


def run_pairs(i, j):
    grid = jax.ShapeDtypeStruct((2, 6912, 128), jnp.float32)
    vm = pl.BlockSpec(memory_space=pltpu.VMEM)
    an = pl.BlockSpec(memory_space=pl.ANY)
    return pl.pallas_call(
        exchange,
        out_shape=[grid, grid],
        in_specs=[an, an] + [vm] * 6,
        out_specs=[an, an],
        scratch_shapes=[pltpu.VMEM((2, 6912, 128), jnp.float32)] * 4
        + [pltpu.VMEM((96 * 97, 128), jnp.float32), pltpu.SemaphoreType.DMA((4,))],
        compiler_params=pltpu.CompilerParams(vmem_limit_bytes=62 * 1024 * 1024),
    )(i, j, kernel_table(), *tables())


def local(orbitals):
    own = orbitals.reshape(8, 6, 72, 128)
    mine = lax.all_to_all(own.reshape(4, 2, 6, 72, 128), ("zl", "c"), 0, 0)
    mine = lax.all_gather(mine, "x").reshape(4, 2, 2, 2, 6, 72, 128)
    i = mine.transpose(3, 1, 0, 2, 4, 5, 6).reshape(2, 6912, 128)
    partners = lax.all_gather(own[0:2], ("y", "zh"))[0:4]
    partners = lax.all_to_all(partners, "x", 0, 0)
    partners = lax.all_gather(partners, ("zl", "c")).reshape(2, 2, 4, 2, 6, 72, 128)
    j = partners.transpose(3, 0, 2, 1, 4, 5, 6).reshape(2, 6912, 128)
    near, far = run_pairs(i, j)
    near = near.reshape(2, 2, 4, 2, 6, 72, 128).transpose(2, 1, 3, 0, 4, 5, 6)
    near = lax.psum_scatter(near, "x", scatter_dimension=0).reshape(4, 2, 6, 72, 128)
    near = lax.all_to_all(near, ("zl", "c"), 0, 0).reshape(8, 6, 72, 128)
    far = far.reshape(2, 2, 4, 2, 6, 72, 128).transpose(1, 3, 2, 0, 4, 5, 6).reshape(4, 4, 2, 6, 72, 128)
    far = lax.psum_scatter(far, ("zl", "c"), scatter_dimension=0)
    far = lax.all_to_all(far, "x", 0, 0)
    far = lax.psum(far, ("y", "zh"))
    band = lax.axis_index(("y", "zh"))
    extra = sum(jnp.where(band == r, far[r], 0.0) for r in range(4))
    out = near.at[0:2].add(extra)
    return out.reshape(8, 6, 9216)


def solution(mesh):
    fine = jax.sharding.Mesh(mesh.devices.reshape(4, 2, 2, 4, 2), ("y", "zh", "zl", "x", "c"))
    placed = P(("y", "zh"), ("zl", "x", "c"), None)
    return jax.shard_map(local, mesh=fine, in_specs=(placed,), out_specs=placed, check_vma=False)
```

time: 890 us -> 699 us (0.79)
  waiting for transfers between devices: 585 us -> 428 us
  matrix products: 144 us -> 0 us
  blocking collectives: 0 us -> 112 us
  Pallas kernels: 0 us -> 99.7 us
  local copies, waits for them, and re-layouts: 79.6 us -> 33.8 us
  starting transfers between devices: 37.9 us -> 3.79 us
  other arithmetic: 25.4 us -> 6.74 us
    all_to_all x8 -> x1, waiting for transfers between devices: 345 us -> 54.8 us  [local(): near = lax.all_to_all(near, ('zl', 'c'), 0, 0).reshape(8, 6, 72, 128)]
    psum x2 -> x1, waiting for transfers between devices: 240 us -> 51.4 us  [local(): far = lax.psum(far, ('y', 'zh'))]
    dot_general x24 -> x0, matrix products: 144 us -> none  [the longest x4 28.7 us: coulomb_solve(): jnp.einsum('pxyz,xu->puyz', field, table, precision=HIGHEST) * kernel]
    all_gather x0 -> x3, waiting for transfers between devices: none -> 137 us  [the longest x1 61.8 us: local(): lax.all_gather(partners, ('zl', 'c')).reshape(2, 2, 4, 2, 6, 72, 128)]
    unnamed x2 -> x7, waiting for transfers between devices: 0.03 us -> 114 us
    all_to_all x0 -> x3, blocking collectives: none -> 112 us  [the longest x1 41.6 us: local(): far = lax.all_to_all(far, 'x', 0, 0)]
    pallas_call x0 -> x1, Pallas kernels: none -> 99.7 us  [run_pairs(): pl.pallas_call(exchange, out_shape=[grid, grid], in_specs=[an, an] + [vm]...]
    reduce_scatter x0 -> x1, waiting for transfers between devices: none -> 70.4 us  [local(): far = lax.psum_scatter(far, ('zl', 'c'), scatter_dimension=0)]
  transfers between devices with their start and end apart: 10 -> 7, of which waited for: 10 -> 7; matrix products, arithmetic and copies ran while one was open for 19% -> 3% of each run, Pallas kernels for 0% -> 0%
where the time goes in v1:
time: 699 us; the launch traced here: 697 us
  waiting for transfers between devices  428 us (61%)
  blocking collectives  112 us (16%)
  Pallas kernels  99.7 us (14%)
  local copies, waits for them, and re-layouts  33.8 us (5%)
  between operations  13.6 us (2%)
    unnamed x7, waiting for transfers between devices  114 us
    pallas_call x1, Pallas kernels, run_pairs(): pl.pallas_call(exchange, out_shape=[grid, grid], in_specs=[an, an] + [vm]...  99.7 us
    reduce_scatter x1, waiting for transfers between devices, local(): far = lax.psum_scatter(far, ('zl', 'c'), scatter_dimension=0)  70.4 us
    all_gather x1, waiting for transfers between devices, local(): lax.all_gather(partners, ('zl', 'c')).reshape(2, 2, 4, 2, 6, 72, 128)  61.8 us
    all_to_all x1, waiting for transfers between devices, local(): near = lax.all_to_all(near, ('zl', 'c'), 0, 0).reshape(8, 6, 72, 128)  54.8 us
    psum x1, waiting for transfers between devices, local(): far = lax.psum(far, ('y', 'zh'))  51.4 us
    all_to_all x1, blocking collectives, local(): far = lax.all_to_all(far, 'x', 0, 0)  41.6 us
    all_to_all x1, blocking collectives, local(): partners = lax.all_to_all(partners, 'x', 0, 0)  40.3 us
  transfers between devices with their start and end apart: 7, of which 7 were waited for; matrix products, arithmetic and copies ran while one was open for 3% of the time, Pallas kernels for 0%

profile of v1, /device:TPU:8, one launch (start us, length us, event | category | flops | bytes accessed | tf_op | source)
XLA Modules:
  0.0 697.2 jit_solution(17467838573758361281)
XLA Ops:
  6.5 0.0 all-gather.6.cloned.1.call-start
  6.5 1.6 slice.49
  8.1 0.4 all_gather.20
  8.5 0.8 copy.33
  9.3 0.0 all-gather.6.cloned.1.call-update
  9.3 0.0 all-gather.8.cloned.1.call-start
  9.4 1.8 copy.40
  11.2 0.1 copy.30
  11.3 29.9 %all_to_all.20 = f32[4,2,6,72,128]{4,3,1,2,0:T(8,128)S(1)} all-to-all(f32[4,2,6,72,128]{4,3,1,2,0:T(8,128)S(1)} %copy.30), channel_id=1, replica_groups=mesh['y'=4,'zh'=2,'zl'=2,'x'=4,'c'=2] {'zl','c'}, dimensions={0} | all-to-all | bytes 3538944 | tf_op jit(solution)/shard_map/all_to_all | solution.py:166
  41.2 1.3 copy.31
  42.5 0.0 all-gather.8.cloned.1.call-update
  42.6 0.0 all-gather.10.cloned.1.call-start
  42.6 37.9 %all-gather.6.cloned.1.call-done = f32[8,2,6,72,128]{4,3,2,1,0:T(8,128)} async-done(((f32[1,2,6,72,128]{4,3,2,1,0:T(8,128)}), f32[8,2,6,72,128]{4,3,2,1,0:T(8,128)}) %all-gather.6.cloned.1.call-update) | async-done | bytes 3538960 | tf_op jit(solution)/shard_map/all_gather | solution.py:169
  80.5 0.0 slice-start
  80.5 1.5 slice-done
  82.0 40.3 %all_to_all.21 = f32[4,2,6,72,128]{4,3,2,1,0:T(8,128)} all-to-all(f32[4,2,6,72,128]{4,3,2,1,0:T(8,128)S(1)} %slice-done), channel_id=1, replica_groups=mesh['y'=4,'zh'=2,'zl'=2,'x'=4,'c'=2] {'x'}, dimensions={0} | all-to-all | bytes 3538944 | tf_op jit(solution)/shard_map/all_to_all | solution.py:170
  122.3 0.0 all-gather.10.cloned.1.call-update
  122.3 0.0 reduce-scatter.5.cloned.1.call-start
  122.4 0.1 add.77
  122.5 0.1 add.78
  122.6 0.1 add.80
  122.7 5.2 fusion.k_ref
  127.9 37.4 %all-gather.8.cloned.1.call-done = f32[16,2,6,72,128]{4,3,2,1,0:T(8,128)} async-done(((f32[4,2,6,72,128]{4,3,2,1,0:T(8,128)}), f32[16,2,6,72,128]{4,3,2,1,0:T(8,128)}) %all-gather.8.cloned.1.call-update) | async-done | bytes 7077904 | tf_op jit(solution)/shard_map/all_gather | solution.py:167
  165.3 6.8 copy.32
  172.1 61.8 %all-gather.10.cloned.1.call-done = f32[16,2,6,72,128]{4,3,2,1,0:T(8,128)} async-done(((f32[4,2,6,72,128]{4,3,2,1,0:T(8,128)}), f32[16,2,6,72,128]{4,3,2,1,0:T(8,128)}) %all-gather.10.cloned.1.call-update) | async-done | bytes 7077904 | tf_op jit(solution)/shard_map/all_gather | solution.py:171
  234.0 6.6 copy.34
  240.6 99.7 %shard_map.64 = (f32[2,6912,128]{2,1,0:T(8,128)}, f32[2,6912,128]{2,1,0:T(8,128)}) custom-call(f32[2,6912,128]{2,1,0:T(8,128)} %bitcast.44, f32[2,6912,128]{2,1,0:T(8,128)} %bitcast.45, f32[9216,128]{1,0:T(8,128)} %fusion.k_ref, bf16[4,256,256]{2,1,0:T(8,128)(2,1)} %constant.78.clone.wz_ref, bf16[4,256,256]{2,1,0:T(8,128)(2,1)} %constant.79.clone.wi_ref, ...), custom_call_target="tpu_custom_call" | custom-call | tf_op jit(solution)/shard_map/pallas_call | solution.py:153
  340.3 6.8 copy.36
  347.1 0.0 reduce-scatter.5.cloned.1.call-update
  347.1 0.0 all-reduce.7.cloned.1.call-start
  347.2 0.0 copy-start
  347.2 0.5 all-reduce.7.cloned.1.call-update
  347.7 0.0 all-reduce.5.cloned.1.call-start
  347.8 70.4 %reduce-scatter.5.cloned.1.call-done = f32[1,4,2,6,72,128]{5,4,3,2,1,0:T(8,128)} async-done(((f32[4,4,2,6,72,128]{5,4,3,2,1,0:T(8,128)}), f32[1,4,2,6,72,128]{5,4,3,2,1,0:T(8,128)}) %reduce-scatter.5.cloned.1.call-update) | async-done | bytes 1769488 | tf_op jit(solution)/shard_map/reduce_scatter | solution.py:178
  418.2 41.6 %all_to_all.22 = f32[4,2,6,72,128]{4,3,2,1,0:T(8,128)} all-to-all(f32[4,2,6,72,128]{4,3,2,1,0:T(8,128)} %bitcast.53), channel_id=1, replica_groups=mesh['y'=4,'zh'=2,'zl'=2,'x'=4,'c'=2] {'x'}, dimensions={0} | all-to-all | bytes 3538944 | tf_op jit(solution)/shard_map/all_to_all | solution.py:179
  459.7 0.0 all-reduce.5.cloned.1.call-update
  459.8 0.0 copy-done
  459.8 0.6 dynamic-slice.8
  460.4 113.4 %all-reduce.7.cloned.1.call-done = f32[4,2,2,2,6,72,128]{6,5,4,2,0,1,3:T(8,128)} async-done(((f32[4,2,2,2,6,72,128]{6,5,4,2,0,1,3:T(8,128)}), f32[4,2,2,2,6,72,128]{6,5,4,2,0,1,3:T(8,128)}) %all-reduce.7.cloned.1.call-update) | async-done | bytes 7077904
  573.8 2.2 constant_dynamic-slice_fusion
  576.0 1.3 copy.35
  577.3 3.6 all-to-all-start.2
  581.0 54.8 %all-to-all-done.2 = f32[4,2,6,72,128]{4,3,2,1,0:T(8,128)S(1)} async-done(((f32[4,2,6,72,128]{4,3,2,1,0:T(8,128)}), f32[4,2,6,72,128]{4,3,2,1,0:T(8,128)S(1)}, u32[]{:S(2)}, u32[]{:S(2)}) %all-to-all-start.2) | async-done | bytes 1769504 | tf_op jit(solution)/shard_map/all_to_all | solution.py:176
  635.7 0.1 copy.43
  635.8 51.4 %all-reduce.5.cloned.1.call-done = f32[4,2,6,72,128]{4,3,2,1,0:T(8,128)} async-done(((f32[4,2,6,72,128]{4,3,2,1,0:T(8,128)}), f32[4,2,6,72,128]{4,3,2,1,0:T(8,128)}) %all-reduce.5.cloned.1.call-update) | async-done | bytes 1769488 | tf_op jit(solution)/shard_map/psum | solution.py:180
  687.2 1.5 fusion.4
  688.7 0.1 copy.37
  688.8 1.5 reshape.146
  (4 shorter events, 0.1 us)
Async XLA Ops:
  6.5 74.0 %all-gather.6.cloned.1.call-start = ((), (), s32[]{:S(2)}) async-start(), calls=%async_computation.5 | async-start | bytes 3981312 | tf_op jit(solution)/shard_map/all_gather | solution.py:169
  9.3 156.0 %all-gather.8.cloned.1.call-start = ((), (), s32[]{:S(2)}) async-start(), calls=%async_computation.8 | async-start | bytes 8847360 | tf_op jit(solution)/shard_map/all_gather | solution.py:167
  42.6 191.4 %all-gather.10.cloned.1.call-start = ((), (), s32[]{:S(2)}) async-start(), calls=%async_computation.9 | async-start | bytes 8847360 | tf_op jit(solution)/shard_map/all_gather | solution.py:171
  80.5 1.5 slice-start
  122.3 295.8 %reduce-scatter.5.cloned.1.call-start = ((), (), s32[]{:S(2)}) async-start(), calls=%async_computation.6 | async-start | bytes 8847360 | tf_op jit(solution)/shard_map/reduce_scatter | solution.py:178
  347.1 226.6 %all-reduce.7.cloned.1.call-start = ((), (), s32[]{:S(2)}) async-start(), calls=%async_computation.10 | async-start | bytes 14155776
  347.2 112.6 %copy-start = (u32[128]{0:T(128)S(1)}, u32[128]{0:T(128)}, u32[]{:S(2)}) copy-start(u32[128]{0:T(128)} %constant.88) | copy-start | bytes 1540
  347.7 339.5 %all-reduce.5.cloned.1.call-start = ((), (), s32[]{:S(2)}) async-start(), calls=%async_computation.7 | async-start | bytes 3538944 | tf_op jit(solution)/shard_map/psum | solution.py:180
  577.3 58.4 %all-to-all-start.2 = ((f32[4,2,6,72,128]{4,3,2,1,0:T(8,128)}), f32[4,2,6,72,128]{4,3,2,1,0:T(8,128)S(1)}, u32[]{:S(2)}, u32[]{:S(2)}) async-start(f32[4,2,6,72,128]{4,3,2,1,0:T(8,128)} %bitcast.17), calls=%async_computation.2 | async-start | bytes 3538944 | tf_op jit(solution)/shard_map/all_to_all | solution.py:176
Sparse Core Ops, SparseCore 0:
  9.7 70.7 all-gather.5
  82.2 83.1 all-gather.7
  167.0 66.9 all-gather.9
  347.3 70.8 reduce-scatter.4
  420.4 153.3 all-reduce.6
  576.2 110.9 all-reduce.4

commit v2 on v1

--- a/solution.py
+++ b/solution.py
@@ -73,7 +73,7 @@
     o = dot(jnp.concatenate([hi, lo], axis=1), w)
     return o[:, :128] + o[:, 128:]
 
-def pair(i_ref, j_ref, near_ref, far_ref, a_ref, k_ref, wz_ref, wi_ref, ty_ref, tyi_ref, tx_ref, near_first, far_first, XB=8, VB=4, AS=96, stages=7):
+def pair(i_ref, j_ref, near_ref, far_ref, a_ref, k_ref, wz_ref, wi_ref, ty_ref, tyi_ref, tx_ref, near_first, far_first, XB=8, VB=4, AS=96, stages=7, hooks=None):
     lane = lax.broadcasted_iota(jnp.int32, (24*XB, 128), 1)
     def fwd(xb, _):
         base = xb*(XB*72)
@@ -94,6 +94,8 @@
         return 0
     if stages & 1:
         lax.fori_loop(0, 96//XB, fwd, 0)
+    if hooks:
+        hooks[0]()
     def mid(vb, _):
         for vv in range(0, VB, 2):
             v = vb*VB+vv
@@ -105,6 +107,8 @@
         return 0
     if stages & 2:
         lax.fori_loop(0, 96//VB, mid, 0)
+    if hooks:
+        hooks[1]()
     def inv(xb, _):
         parts = [[] for _ in range(4)]
         for xx in range(0, XB, 2):
@@ -128,59 +132,341 @@
         lax.fori_loop(0, 96//XB, inv, 0)
 
 
-def exchange(i_hbm, j_hbm, k_ref, wz_ref, wi_ref, ty_ref, tyi_ref, tx_ref, near, far, iv, jv, nv, fv, a, sem):
+MESH = pl.DeviceIdType.MESH
+PIECE = 432
+
+
+class Comm:
+    def __init__(self, ss, rs):
+        self.ss, self.rs, self.sent, self.n, self.r = ss, rs, [], 0, 0
+
+    def slot(self, count=1):
+        self.r += count
+        return self.r - count
+
+    def send(self, src, dst, recv, device, when=None):
+        copy = pltpu.make_async_remote_copy(src_ref=src, dst_ref=dst, send_sem=self.ss.at[self.n], recv_sem=self.rs.at[recv],
+                                            device_id=device, device_id_type=MESH)
+        self.n += 1
+        self.sent.append((copy, when))
+        guarded(when, copy.start)
+
+    def wait(self, ref, recv):
+        pltpu.make_async_copy(ref, ref, self.rs.at[recv]).wait()
+
+    def finish(self):
+        for copy, when in self.sent:
+            guarded(when, copy.wait_send)
+
+
+def guarded(when, do):
+    if when is None:
+        do()
+    else:
+        pl.when(when)(lambda: do())
+
+
+def piece(zl, x, c):
+    return pl.ds(pl.multiple_of((zl * 8 + x * 2 + c) * PIECE, PIECE), PIECE)
+
+
+def exchange(o, k_ref, wz_ref, wi_ref, ty_ref, tyi_ref, tx_ref, out, extra, iv, jv, nv, fv, a, fw, rb, db, zb, zc, yb, ss, rs, ls):
+    y, zh, zl, x, c = (lax.axis_index(n) for n in ("y", "zh", "zl", "x", "c"))
+    xs = [lax.rem(x + d, 4) for d in range(4)]
+    ys = [lax.rem(y + d, 4) for d in range(4)]
+    own = 2 * zl + c
+    quad = [(zl if k < 2 else 1 - zl, c if k % 2 == 0 else 1 - c) for k in range(4)]
+    in_root_zh = zh == lax.rem(x, 2)
+    off_root_zh = jnp.logical_not(in_root_zh)
+    dy = lax.rem(y + 4 - lax.div(x, 2), 4)
+    root = in_root_zh & (dy == 0)
+    branch = in_root_zh & (dy != 0)
+    prim = jnp.where(in_root_zh, zl, 1 - zl)
+    band = 2 * y + zh
+    gives = y < 2
+    dx_root = lax.rem(x + 8 - band, 4)
+
+    def at(y=y, zh=zh, zl=zl, x=x, c=c):
+        return (y, zh, zl, x, c)
+
+    barrier = pltpu.get_barrier_semaphore()
+    zn = (1 - zh, 1 - zl)
+    friends = [at(x=xs[1]), at(x=xs[2]), at(x=xs[3]), at(y=ys[1]), at(y=ys[3]), at(zh=zn[0], zl=zn[1])]
+    friends += [at(zl=qz, c=qc) for qz, qc in quad[1:]]
+    for f in friends:
+        pl.semaphore_signal(barrier, inc=1, device_id=f, device_id_type=MESH)
+    pl.semaphore_wait(barrier, len(friends))
+
+    m = Comm(ss, rs)
+    S1 = [[m.slot() for _ in range(4)] for _ in range(2)]
+    S2 = [[[m.slot() for _ in range(4)] for _ in range(2)] for _ in range(2)]
+    S3 = [[[m.slot() for _ in range(2)] for _ in range(2)] for _ in range(2)]
+    J1 = [m.slot(4) for _ in range(2)]
+    YM, ZAB, SEC = ([[m.slot() for _ in range(4)] for _ in range(2)] for _ in range(3))
+    DIE = [[[m.slot() for _ in range(4)] for _ in range(2)] for _ in range(2)]
+    keep = [pltpu.make_async_copy(o.at[2 * own + g], iv.at[g, piece(zl, x, c)], ls.at[g]) for g in range(2)]
+    root_keep = [pltpu.make_async_copy(o.at[g], jv.at[g, piece(zl, x, c)], ls.at[2 + g]) for g in range(2)]
+
+    def i_first(g):
+        for k in range(1, 4):
+            qz, qc = quad[k]
+            m.send(o.at[2 * (2 * qz + qc) + g], iv.at[g, piece(zl, x, c)], S1[g][k], at(zl=qz, c=qc))
+        keep[g].start()
+
+    def i_spread(g, k):
+        rows = piece(quad[k][0], x, quad[k][1])
+        src = iv.at[g, rows]
+        if k == 0:
+            src = o.at[2 * own + g]
+        else:
+            m.wait(src, S1[g][k])
+        for d in range(2):
+            m.send(src, iv.at[g, rows], S2[g][d][k], at(x=xs[1 + 2 * d]))
+
+    def i_forward(g):
+        for kk in range(2):
+            for d in range(2):
+                k = kk + 2 * d
+                rows = iv.at[g, piece(quad[k][0], xs[3 - 2 * d], quad[k][1])]
+                m.wait(rows, S2[g][d][k])
+                m.send(rows, rows, S3[g][d][kk], at(x=xs[1 + 2 * d]))
+
+    def i_finish(g):
+        keep[g].wait()
+        rows = iv.at[g, pl.ds(0, PIECE)]
+        for d in range(2):
+            for kk in range(2):
+                m.wait(rows, S2[g][d][kk + 2 - 2 * d])
+                m.wait(rows, S3[g][d][kk])
+
+    def j_first(g):
+        m.send(o.at[g], jv.at[g, piece(zl, x, c)], J1[g] + dx_root, at(x=band), gives & (dx_root != 0))
+        guarded(root, root_keep[g].start)
+
+    def j_primary(g):
+        for dx in range(4):
+            rows = jv.at[g, piece(prim, xs[dx], c)]
+            guarded(root, root_keep[g].wait if dx == 0 else lambda: m.wait(rows, J1[g] + dx))
+            guarded(branch, lambda: m.wait(rows, YM[g][dx]))
+            guarded(off_root_zh, lambda: m.wait(rows, ZAB[g][dx]))
+            m.send(rows, rows, YM[g][dx], at(y=ys[1]), root | (branch & (dy == 1)) if dx < 2 else root)
+            m.send(rows, rows, YM[g][dx], at(y=ys[3]), root | (branch & (dy == 3)) if dx >= 2 else root)
+            m.send(rows, rows, ZAB[g][dx], at(zh=zn[0], zl=zn[1]), in_root_zh)
+            m.send(rows, rows, SEC[g][dx], at(zl=1 - zl))
+            m.send(rows, rows, DIE[g][0][dx], at(c=1 - c))
+
+    def j_secondary(g):
+        for dx in range(4):
+            rows = jv.at[g, piece(1 - prim, xs[dx], c)]
+            m.wait(rows, SEC[g][dx])
+            m.send(rows, rows, DIE[g][1][dx], at(c=1 - c))
+
+    def j_finish(g):
+        for s in range(2):
+            for dx in range(4):
+                m.wait(jv.at[g, pl.ds(0, PIECE)], DIE[g][s][dx])
+
+    R1 = [[[m.slot() for _ in range(2)] for _ in range(2)] for _ in range(2)]
+    R2 = [[[m.slot() for _ in range(4)] for _ in range(2)] for _ in range(2)]
+    R4 = [[m.slot() for _ in range(4)] for _ in range(2)]
+    put = [pltpu.make_async_copy(nv.at[g, piece(zl, x, c)], out.at[2 * own + g], ls.at[4 + g]) for g in range(2)]
+
+    def n_first(g):
+        for kk in range(2):
+            for d in range(2):
+                k = kk + 2 * d
+                m.send(nv.at[g, piece(quad[k][0], xs[2], quad[k][1])], fw.at[g, d, kk], R1[g][d][kk], at(x=xs[1 + 2 * d]))
+        for kk in range(2):
+            for d in range(2):
+                k = kk + 2 - 2 * d
+                rows = nv.at[g, piece(quad[k][0], xs[1 + 2 * d], quad[k][1])]
+                m.send(rows, rows_of(rb, g, d, k), R2[g][d][k], at(x=xs[1 + 2 * d]))
+
+    def rows_of(ref, *index):
+        return ref.at[index]
+
+    def n_second(g):
+        for kk in range(2):
+            for d in range(2):
+                k = kk + 2 * d
+                m.wait(fw.at[g, d, kk], R1[g][d][kk])
+                rows = nv.at[g, piece(quad[k][0], xs[1 + 2 * d], quad[k][1])]
+                rows[...] += fw[g, d, kk]
+                m.send(rows, rb.at[g, d, k], R2[g][d][k], at(x=xs[1 + 2 * d]))
+
+    def n_third(g):
+        for k in (1, 2, 3, 0):
+            rows = nv.at[g, piece(quad[k][0], x, quad[k][1])]
+            m.wait(rb.at[g, 0, k], R2[g][0][k])
+            m.wait(rb.at[g, 1, k], R2[g][1][k])
+            rows[...] += rb[g, 0, k] + rb[g, 1, k]
+            if k == 0:
+                put[g].start()
+            else:
+                m.send(rows, out.at[2 * own + g], R4[g][k], at(zl=quad[k][0], c=quad[k][1]))
+
+    def n_finish(g):
+        for k in range(1, 4):
+            m.wait(out.at[g], R4[g][k])
+        put[g].wait()
+
+    D1 = [[[m.slot() for _ in range(4)] for _ in range(2)] for _ in range(2)]
+    D2, D3 = ([[m.slot() for _ in range(4)] for _ in range(2)] for _ in range(2))
+    D4 = [[[m.slot() for _ in range(4)] for _ in range(2)] for _ in range(2)]
+    D5 = [m.slot() for _ in range(2)]
+    root_put = [pltpu.make_async_copy(fv.at[g, piece(zl, x, c)], extra.at[g], ls.at[6 + g]) for g in range(2)]
+
+    def f_first(g):
+        for s in (1, 0):
+            for dx in range(4):
+                m.send(fv.at[g, piece(prim if s == 0 else 1 - prim, xs[dx], 1 - c)], db.at[g, s, dx], D1[g][s][dx], at(c=1 - c))
+
+    def f_second(g):
+        for dx in range(4):
+            rows = fv.at[g, piece(1 - prim, xs[dx], c)]
+            m.wait(db.at[g, 1, dx], D1[g][1][dx])
+            rows[...] += db[g, 1, dx]
+            m.send(rows, zb.at[g, dx], D2[g][dx], at(zl=1 - zl))
+
+    def f_third(g):
+        for dx in range(4):
+            rows = fv.at[g, piece(prim, xs[dx], c)]
+            m.wait(db.at[g, 0, dx], D1[g][0][dx])
+            m.wait(zb.at[g, dx], D2[g][dx])
+            rows[...] += db[g, 0, dx] + zb[g, dx]
+            m.send(rows, zc.at[g, dx], D3[g][dx], at(zh=zn[0], zl=zn[1]), off_root_zh)
+
+    def f_fourth(g):
+        for dx in (0, 2, 1, 3):
+            rows = fv.at[g, piece(prim, xs[dx], c)]
+
+            def add(ref, slot):
+                m.wait(ref, slot)
+                rows[...] += ref[...]
+
+            near_y, far_y = (0, 1) if dx < 2 else (1, 0)
+            guarded(in_root_zh, lambda: add(zc.at[g, dx], D3[g][dx]))
+            m.send(rows, yb.at[g, near_y, dx], D4[g][near_y][dx], at(y=ys[3 - 2 * near_y]), in_root_zh & (dy == 2))
+
+    def f_fifth(g):
+        for dx in (0, 2, 1, 3):
+            rows = fv.at[g, piece(prim, xs[dx], c)]
+
+            def add(ref, slot):
+                m.wait(ref, slot)
+                rows[...] += ref[...]
+
+            near_y = 0 if dx < 2 else 1
+            guarded(in_root_zh & (dy == 1 + 2 * near_y), lambda: add(yb.at[g, near_y, dx], D4[g][near_y][dx]))
+            for e in range(2):
+                m.send(rows, yb.at[g, e, dx], D4[g][e][dx], at(y=ys[3 - 2 * e]), in_root_zh & (dy == 1 + 2 * e))
+
+    def f_sixth(g):
+        for dx in (0, 2, 1, 3):
+            rows = fv.at[g, piece(prim, xs[dx], c)]
+
+            def add():
+                for e in range(2):
+                    m.wait(yb.at[g, e, dx], D4[g][e][dx])
+                rows[...] += yb[g, 0, dx] + yb[g, 1, dx]
+
+            guarded(root, add)
+            if dx == 0:
+                guarded(root, root_put[g].start)
+            else:
+                m.send(rows, extra.at[g], D5[g], at(x=xs[dx]), root)
+
+    def f_finish(g):
+        guarded(gives & (dx_root != 0), lambda: m.wait(extra.at[g], D5[g]))
+        guarded(root, root_put[g].wait)
+
+    def work(gi, gj, first, second):
+        pair(iv.at[gi], jv.at[gj], nv.at[gi], fv.at[gj], a, k_ref, wz_ref, wi_ref, ty_ref, tyi_ref, tx_ref, gj == gi, gi == 0,
+             AS=97, hooks=(first, second))
+
+    i_first(0)
+    i_spread(0, 0)
+    j_first(0)
+    i_first(1)
+    j_first(1)
+    for k in range(1, 4):
+        i_spread(0, k)
+    i_spread(1, 0)
+    j_primary(0)
+    i_forward(0)
+    for k in range(1, 4):
+        i_spread(1, k)
+    j_secondary(0)
+    j_primary(1)
+    i_finish(0)
+    j_finish(0)
+
+    def in_first():
+        i_forward(1)
+        j_secondary(1)
+
+    work(0, 0, in_first, lambda: None)
+    j_finish(1)
+    work(0, 1, lambda: None, lambda: None)
+    n_first(0)
+    i_finish(1)
+    work(1, 1, lambda: n_second(0), lambda: n_third(0))
+    f_first(1)
+
+    def far_a():
+        f_second(1)
+        f_third(1)
+
+    def far_b():
+        f_fourth(1)
+        f_fifth(1)
+
+    work(1, 0, far_a, far_b)
+    n_first(1)
+    f_first(0)
+    n_second(1)
+    f_second(0)
+    f_third(0)
+    n_third(1)
+    f_fourth(0)
+    f_fifth(0)
+    f_sixth(1)
+    f_sixth(0)
     for g in range(2):
-        pltpu.make_async_copy(i_hbm.at[g], iv.at[g], sem.at[g]).start()
-        pltpu.make_async_copy(j_hbm.at[g], jv.at[g], sem.at[2 + g]).start()
-    for g in range(2):
-        pltpu.make_async_copy(i_hbm.at[g], iv.at[g], sem.at[g]).wait()
-        pltpu.make_async_copy(j_hbm.at[g], jv.at[g], sem.at[2 + g]).wait()
-    for gi, gj in ((0, 0), (0, 1), (1, 1), (1, 0)):
-        pair(iv.at[gi], jv.at[gj], nv.at[gi], fv.at[gj], a, k_ref, wz_ref, wi_ref, ty_ref, tyi_ref, tx_ref,
-             gj == gi, gi == 0, AS=97)
-    for g in range(2):
-        pltpu.make_async_copy(nv.at[g], near.at[g], sem.at[g]).start()
-        pltpu.make_async_copy(fv.at[g], far.at[g], sem.at[2 + g]).start()
-    for g in range(2):
-        pltpu.make_async_copy(nv.at[g], near.at[g], sem.at[g]).wait()
-        pltpu.make_async_copy(fv.at[g], far.at[g], sem.at[2 + g]).wait()
-
-
-def run_pairs(i, j):
-    grid = jax.ShapeDtypeStruct((2, 6912, 128), jnp.float32)
+        n_finish(g)
+        f_finish(g)
+    m.finish()
+
+
+SENDS, RECEIVES = 256, 256
+
+
+def run_pairs(own):
     vm = pl.BlockSpec(memory_space=pltpu.VMEM)
     an = pl.BlockSpec(memory_space=pl.ANY)
+    f32 = jnp.float32
+    big = pltpu.VMEM((2, 6912, 128), f32)
+
+    def pieces(*lead):
+        return pltpu.VMEM(lead + (PIECE, 128), f32)
+
     return pl.pallas_call(
         exchange,
-        out_shape=[grid, grid],
-        in_specs=[an, an] + [vm] * 6,
+        out_shape=[jax.ShapeDtypeStruct((8, PIECE, 128), f32), jax.ShapeDtypeStruct((2, PIECE, 128), f32)],
+        in_specs=[an] + [vm] * 6,
         out_specs=[an, an],
-        scratch_shapes=[pltpu.VMEM((2, 6912, 128), jnp.float32)] * 4
-        + [pltpu.VMEM((96 * 97, 128), jnp.float32), pltpu.SemaphoreType.DMA((4,))],
-        compiler_params=pltpu.CompilerParams(vmem_limit_bytes=62 * 1024 * 1024),
-    )(i, j, kernel_table(), *tables())
+        scratch_shapes=[big] * 4
+        + [pltpu.VMEM((96 * 97, 128), f32), pieces(2, 2, 2), pieces(2, 2, 4), pieces(2, 2, 4), pieces(2, 4), pieces(2, 4), pieces(2, 2, 4)]
+        + [pltpu.SemaphoreType.DMA((SENDS,)), pltpu.SemaphoreType.DMA((RECEIVES,)), pltpu.SemaphoreType.DMA((8,))],
+        compiler_params=pltpu.CompilerParams(vmem_limit_bytes=67043328, collective_id=1, has_side_effects=True),
+    )(own, kernel_table(), *tables())
 
 
 def local(orbitals):
-    own = orbitals.reshape(8, 6, 72, 128)
-    mine = lax.all_to_all(own.reshape(4, 2, 6, 72, 128), ("zl", "c"), 0, 0)
-    mine = lax.all_gather(mine, "x").reshape(4, 2, 2, 2, 6, 72, 128)
-    i = mine.transpose(3, 1, 0, 2, 4, 5, 6).reshape(2, 6912, 128)
-    partners = lax.all_gather(own[0:2], ("y", "zh"))[0:4]
-    partners = lax.all_to_all(partners, "x", 0, 0)
-    partners = lax.all_gather(partners, ("zl", "c")).reshape(2, 2, 4, 2, 6, 72, 128)
-    j = partners.transpose(3, 0, 2, 1, 4, 5, 6).reshape(2, 6912, 128)
-    near, far = run_pairs(i, j)
-    near = near.reshape(2, 2, 4, 2, 6, 72, 128).transpose(2, 1, 3, 0, 4, 5, 6)
-    near = lax.psum_scatter(near, "x", scatter_dimension=0).reshape(4, 2, 6, 72, 128)
-    near = lax.all_to_all(near, ("zl", "c"), 0, 0).reshape(8, 6, 72, 128)
-    far = far.reshape(2, 2, 4, 2, 6, 72, 128).transpose(1, 3, 2, 0, 4, 5, 6).reshape(4, 4, 2, 6, 72, 128)
-    far = lax.psum_scatter(far, ("zl", "c"), scatter_dimension=0)
-    far = lax.all_to_all(far, "x", 0, 0)
-    far = lax.psum(far, ("y", "zh"))
-    band = lax.axis_index(("y", "zh"))
-    extra = sum(jnp.where(band == r, far[r], 0.0) for r in range(4))
-    out = near.at[0:2].add(extra)
+    own = orbitals.reshape(8, PIECE, 128)
+    near, far = run_pairs(own)
+    gives = lax.axis_index("y") < 2
+    out = near.at[0:2].add(jnp.where(gives, far, 0.0))
     return out.reshape(8, 6, 9216)
 
 

time: 699 us -> 279 us (0.40)
  waiting for transfers between devices: 428 us -> 0 us
  Pallas kernels: 99.7 us -> 258 us
  blocking collectives: 112 us -> 0 us
  local copies, waits for them, and re-layouts: 33.8 us -> 8.39 us
  between operations: 13.6 us -> 0.05 us
    pallas_call x1, Pallas kernels: 99.7 us -> 258 us  [run_pairs(): pl.pallas_call(exchange, out_shape=[jax.ShapeDtypeStruct((8, PIECE, 128),...]
    all_gather x3 -> x0, waiting for transfers between devices: 137 us -> none  [the longest x1 61.8 us: local(): lax.all_gather(partners, ('zl', 'c')).reshape(2, 2, 4, 2, 6, 72, 128)]
    unnamed x7 -> x0, waiting for transfers between devices: 114 us -> none
    all_to_all x3 -> x0, blocking collectives: 112 us -> none  [the longest x1 41.6 us: local(): far = lax.all_to_all(far, 'x', 0, 0)]
    reduce_scatter x1 -> x0, waiting for transfers between devices: 70.4 us -> none  [local(): far = lax.psum_scatter(far, ('zl', 'c'), scatter_dimension=0)]
    all_to_all x1 -> x0, waiting for transfers between devices: 54.8 us -> none  [local(): near = lax.all_to_all(near, ('zl', 'c'), 0, 0).reshape(8, 6, 72, 128)]
    psum x1 -> x0, waiting for transfers between devices: 51.4 us -> none  [local(): far = lax.psum(far, ('y', 'zh'))]
    transpose x2 -> x0, local copies, waits for them, and re-layouts: 13.4 us -> none  [the longest x1 6.79 us: local(): i = mine.transpose(3, 1, 0, 2, 4, 5, 6).reshape(2, 6912, 128)]
  transfers between devices with their start and end apart: 7 -> 0, of which waited for: 7 -> 0; matrix products, arithmetic and copies ran while one was open for 3% -> 0% of each run, Pallas kernels for 0% -> 0%
where the time goes in v2:
time: 279 us; the launch traced here: 274 us
  Pallas kernels  258 us (92%)
  local copies, waits for them, and re-layouts  8.39 us (3%)
  other arithmetic  7.12 us (3%)
    pallas_call x1, Pallas kernels, run_pairs(): pl.pallas_call(exchange, out_shape=[jax.ShapeDtypeStruct((8, PIECE, 128),...  258 us

profile of v2, /device:TPU:8, one launch (start us, length us, event | category | flops | bytes accessed | tf_op | source)
XLA Modules:
  0.0 273.9 jit_solution(11726382694459696144)
XLA Ops:
  0.0 2.5 copy.9
  2.5 1.6 reshape.90.o
  4.2 0.1 add.54
  4.2 0.1 add.55
  4.4 0.1 add.57
  4.5 5.1 %fusion.k_ref = f32[9216,128]{1,0:T(8,128)} fusion(f32[128]{0:T(128)S(1)} %pad.6, f32[9216]{0:T(1024)S(1)} %add.58), kind=kLoop, calls=%fused_computation.2 | loop fusion | flops 12976128 | bytes 4755968 | tf_op jit(solution)/shard_map/mul | solution.py:56
  9.6 258.3 %shard_map.64 = (f32[8,432,128]{2,1,0:T(8,128)}, f32[2,432,128]{2,1,0:T(8,128)}) custom-call(f32[8,432,128]{2,1,0:T(8,128)} %reshape.90.o, f32[9216,128]{1,0:T(8,128)} %fusion.k_ref, bf16[4,256,256]{2,1,0:T(8,128)(2,1)} %constant.68.clone.wz_ref, bf16[4,256,256]{2,1,0:T(8,128)(2,1)} %constant.69.clone.wi_ref, bf16[192,192]{1,0:T(8,128)(2,1)} %constant.70.clone.ty_ref, ...), custom_call_target="tpu_custom_call" | custom-call | tf_op jit(solution)/shard_map/pallas_call | solution.py:453
  267.9 2.0 add_dynamic-update-slice_fusion
  269.9 1.7 reshape.91
  271.6 2.2 copy.10
  (4 shorter events, 0.1 us)

commit v3 on v2

v3 whole, which is shorter than its diff:
```python
import math, functools
import numpy as np
import jax, jax.numpy as jnp
from jax import lax
from jax.experimental import pallas as pl
from jax.experimental.pallas import tpu as pltpu
from jax.sharding import PartitionSpec as P
import ml_dtypes

N = 96
OMEGA = 0.106
CELL = 41.05
bf = jnp.bfloat16
XB, VB, AS = 24, 24, 97

def split_np(t):
    t = t.astype(np.float32)
    hi = t.astype(ml_dtypes.bfloat16)
    lo = (t - hi.astype(np.float32)).astype(ml_dtypes.bfloat16)
    return hi, lo

def tables():
    k = np.arange(N)
    ang = 2*np.pi*((k[:,None]*k[None,:])%N)/N
    T = np.cos(ang)+np.sin(ang)
    hi, lo = split_np(T)
    wz = np.zeros((4,256,256), ml_dtypes.bfloat16)
    wi = np.zeros((4,256,256), ml_dtypes.bfloat16)
    for l in range(4):
        lane = (96*l + np.arange(N)) % 128
        wz[l, lane, 0:96] = hi
        wz[l, lane, 128:224] = lo
        wz[l, 128+lane, 0:96] = hi
        wi[l, 0:96, lane] = hi.T
        wi[l, 0:96, 128+lane] = lo.T
        wi[l, 128:224, lane] = hi.T
    def two(hi, lo):
        t = np.zeros((192,192), ml_dtypes.bfloat16)
        t[:96,:96]=hi; t[:96,96:]=hi; t[96:,:96]=lo
        return t
    order = np.array([4*kk+l for l in range(4) for kk in range(24)])
    ty = two(hi[:,order], lo[:,order])
    tyi = two(hi[order,:], lo[order,:])
    tx = two(hi, lo)
    return wz, wi, ty, tyi, tx

def kernel_table():
    idx = jnp.arange(N, dtype=jnp.int32)
    f = jnp.where(idx <= N//2, idx, idx-N).astype(jnp.float32)
    sq = f*f
    sqw = jnp.pad(sq, (0,32))
    g2 = (2.0*math.pi/CELL)**2 * (sq[:,None,None]+sq[None,:,None]+sqw[None,None,:])
    pos = g2 > 0
    safe = jnp.where(pos, g2, 1.0)
    val = 4.0*math.pi/safe * -jnp.expm1(-safe/(4.0*OMEGA*OMEGA))
    val = jnp.where(pos, val, math.pi/(OMEGA*OMEGA))
    return (val * (-0.25/float(N**3))).reshape(N*N, 128)

def split(x):
    hi = x.astype(bf)
    lo = (x - hi.astype(jnp.float32)).astype(bf)
    return hi, lo

def dot(a, b):
    return lax.dot_general(a, b, (((1,),(0,)),((),())), preferred_element_type=jnp.float32)

def left(t, x):
    hi, lo = split(x)
    q = dot(t, jnp.concatenate([hi, lo], axis=0))
    return q[:96] + q[96:]

def right(x, w):
    hi, lo = split(x)
    o = dot(jnp.concatenate([hi, lo], axis=1), w)
    return o[:, :128] + o[:, 128:]


def transform_pairs(iv, jv, nv, fv, a_ref, k_ref, wz_ref, wi_ref, ty_ref, tyi_ref, tx_ref, point):
    lane = lax.broadcasted_iota(jnp.int32, (24 * XB, 128), 1)

    def one(t, _):
        gi = t // 2
        gj = ((t + 1) // 2) % 2
        i_ref, j_ref, near_ref, far_ref = iv.at[gi], jv.at[gj], nv.at[gi], fv.at[gj]
        near_first, far_first = gi == gj, gi == 0
        point(t, 0)

        def fwd(xb, _):
            base = xb * (XB * 72)
            d = []
            for s in range(3):
                rows = pl.ds(base + s, 24 * XB, stride=3)
                d.append(i_ref[rows, :] * j_ref[rows, :])
            m = [d[0], jnp.where(lane >= 96, d[0], d[1]), jnp.where(lane >= 64, d[1], d[2]), d[2]]
            o = [right(m[l], wz_ref[l]) for l in range(4)]
            for xx in range(0, XB, 2):
                cols = []
                for x in (xx, xx + 1):
                    cols.append(jnp.concatenate([o[l][24 * x:24 * x + 24] for l in range(4)], axis=0))
                q = left(ty_ref[...], jnp.concatenate(cols, axis=1))
                row = (xb * XB + xx) * AS
                a_ref[pl.ds(row, 96), :] = q[:, :128]
                a_ref[pl.ds(row + AS, 96), :] = q[:, 128:]
            return 0

        lax.fori_loop(0, 96 // XB, fwd, 0)
        point(t, 1)

        def mid(vb, _):
            for vv in range(0, VB, 2):
                v = vb * VB + vv
                b = jnp.concatenate([a_ref[pl.ds(v, 96, stride=AS), :], a_ref[pl.ds(v + 1, 96, stride=AS), :]], axis=1)
                kk = jnp.concatenate([k_ref[pl.ds(v * 96, 96), :], k_ref[pl.ds(v * 96 + 96, 96), :]], axis=1)
                b = left(tx_ref[...], left(tx_ref[...], b) * kk)
                a_ref[pl.ds(v, 96, stride=AS), :] = b[:, :128]
                a_ref[pl.ds(v + 1, 96, stride=AS), :] = b[:, 128:]
            return 0

        lax.fori_loop(0, 96 // VB, mid, 0)
        point(t, 2)

        def inv(xb, _):
            parts = [[] for _ in range(4)]
            for xx in range(0, XB, 2):
                row = (xb * XB + xx) * AS
                b = jnp.concatenate([a_ref[pl.ds(row, 96), :], a_ref[pl.ds(row + AS, 96), :]], axis=1)
                q = left(tyi_ref[...], b)
                for x in range(2):
                    for l in range(4):
                        parts[l].append(q[24 * l:24 * l + 24, 128 * x:128 * x + 128])
            o = [right(jnp.concatenate(parts[l], axis=0), wi_ref[l]) for l in range(4)]
            vs = [jnp.where(lane < 96, o[0], o[1]), jnp.where(lane < 64, o[1], o[2]), jnp.where(lane < 32, o[2], o[3])]
            base = xb * (XB * 72)
            for s in range(3):
                rows = pl.ds(base + s, 24 * XB, stride=3)
                near_ref[rows, :] = jnp.where(near_first, 0.0, near_ref[rows, :]) + j_ref[rows, :] * vs[s]
                far_ref[rows, :] = jnp.where(far_first, 0.0, far_ref[rows, :]) + i_ref[rows, :] * vs[s]
            return 0

        lax.fori_loop(0, 96 // XB, inv, 0)
        return 0

    lax.fori_loop(0, 4, one, 0)


MESH = pl.DeviceIdType.MESH
PIECE = 432


class Comm:
    def __init__(self, ss, rs, some):
        self.ss, self.rs, self.some, self.sent, self.n, self.r = ss, rs, some, [], 0, 0

    def slot(self):
        self.r += 1
        return self.r - 1

    def send(self, src, dst, recv, device, when=None):
        copy = pltpu.make_async_remote_copy(src_ref=src, dst_ref=dst, send_sem=self.ss.at[self.n], recv_sem=self.rs.at[recv],
                                            device_id=device, device_id_type=MESH)
        self.n += 1
        self.sent.append(when)
        guarded(when, copy.start)

    def wait(self, recv):
        pltpu.make_async_copy(self.some, self.some, self.rs.at[recv]).wait()

    def finish(self):
        for n, when in enumerate(self.sent):
            guarded(when, pltpu.make_async_copy(self.some, self.some, self.ss.at[n]).wait)


def guarded(when, do):
    if when is None:
        do()
    else:
        pl.when(when)(lambda: do())


def piece(zl, x, c):
    return pl.ds(pl.multiple_of((zl * 8 + x * 2 + c) * PIECE, PIECE), PIECE)


def exchange(o, k_ref, wz_ref, wi_ref, ty_ref, tyi_ref, tx_ref, out, extra, iv, jv, nv, fv, a, fw, rb, db, zb, zc, yb, ss, rs, ls):
    y, zh, zl, x, c = (lax.axis_index(n) for n in ("y", "zh", "zl", "x", "c"))
    xs = [lax.rem(x + d, 4) for d in range(4)]
    ys = [lax.rem(y + d, 4) for d in range(4)]
    own = 2 * zl + c
    quad = [(zl if k < 2 else 1 - zl, c if k % 2 == 0 else 1 - c) for k in range(4)]
    root_y, root_zh = lax.div(x, 2), lax.rem(x, 2)
    dy = lax.rem(y + 4 - root_y, 4)
    in_root_zh = zh == root_zh
    home = [in_root_zh, jnp.logical_not(in_root_zh)]
    away = [home[1], home[0]]
    prim = jnp.where(in_root_zh, zl, 1 - zl)
    band = 2 * y + zh
    gives = y < 2
    shift = lax.rem(x + 8 - band, 4)
    units = [lax.rem(x + dy + j, 4) for j in range(4)]

    def at(y=y, zh=zh, zl=zl, x=x, c=c):
        return (y, zh, zl, x, c)

    entry = [at(x=lax.rem(band, 4), y=lax.rem(y + shift, 4)), at(x=lax.rem(band, 4), y=lax.rem(y + shift, 4), zh=1 - zh, zl=1 - zl)]
    source = at(x=units[0], y=root_y, zh=root_zh, zl=prim)
    at_home_0 = jnp.logical_and(in_root_zh, dy == 0)
    gives_away = [jnp.logical_and(gives, shift != 0), gives]
    takes = [jnp.logical_and(in_root_zh, dy != 0), home[1]]
    gets = jnp.logical_not(at_home_0)

    barrier = pltpu.get_barrier_semaphore()
    cross = at(zh=1 - zh, zl=1 - zl)
    friends = [at(x=xs[1]), at(x=xs[2]), at(x=xs[3]), at(y=ys[1]), at(y=ys[3]), cross]
    friends += [at(zl=qz, c=qc) for qz, qc in quad[1:]]
    for f in friends:
        pl.semaphore_signal(barrier, inc=1, device_id=f, device_id_type=MESH)
    for g in range(2):
        guarded(gives_away[g], lambda: pl.semaphore_signal(barrier, inc=1, device_id=entry[g], device_id_type=MESH))
    guarded(gets, lambda: pl.semaphore_signal(barrier, inc=1, device_id=source, device_id_type=MESH))
    count = gets.astype(jnp.int32) + gives_away[0].astype(jnp.int32) + gives_away[1].astype(jnp.int32)
    pl.semaphore_wait(barrier, len(friends) + count)

    m = Comm(ss, rs, fw.at[0, 0, 0])

    def slots(*shape):
        return [slots(*shape[1:]) for _ in range(shape[0])] if shape else m.slot()

    S1, S2, S3 = slots(2, 4), slots(2, 2, 4), slots(2, 2, 2)
    J1, YM, ZAB, SEC, DIE = slots(2), slots(2, 4), slots(2, 4), slots(2, 4), slots(2, 2, 4)
    keep = [pltpu.make_async_copy(o.at[2 * own + g], iv.at[g, piece(zl, x, c)], ls.at[g]) for g in range(2)]
    root_keep = pltpu.make_async_copy(o.at[0], jv.at[0, piece(zl, x, c)], ls.at[2])

    def i_first(g):
        for k in range(1, 4):
            qz, qc = quad[k]
            m.send(o.at[2 * (2 * qz + qc) + g], iv.at[g, piece(zl, x, c)], S1[g][k], at(zl=qz, c=qc))
        keep[g].start()

    def i_spread(g, k):
        rows = piece(quad[k][0], x, quad[k][1])
        src = iv.at[g, rows]
        if k == 0:
            src = o.at[2 * own + g]
        else:
            m.wait(S1[g][k])
        for d in range(2):
            m.send(src, iv.at[g, rows], S2[g][d][k], at(x=xs[1 + 2 * d]))

    def i_forward(g):
        for kk in range(2):
            for d in range(2):
                k = kk + 2 * d
                rows = iv.at[g, piece(quad[k][0], xs[3 - 2 * d], quad[k][1])]
                m.wait(S2[g][d][k])
                m.send(rows, rows, S3[g][d][kk], at(x=xs[1 + 2 * d]))

    def i_finish(g):
        keep[g].wait()
        for d in range(2):
            for kk in range(2):
                m.wait(S2[g][d][kk + 2 - 2 * d])
                m.wait(S3[g][d][kk])

    def j_first(g):
        m.send(o.at[g], jv.at[g, piece(zl, x, c)], J1[g], entry[g], gives_away[g])
        if g == 0:
            guarded(at_home_0, root_keep.start)

    def j_step(g, j):
        rows = jv.at[g, piece(prim, units[j], c)]
        if j == 0:
            if g == 0:
                guarded(at_home_0, root_keep.wait)
            guarded(takes[g], lambda: m.wait(J1[g]))
            for d in range(2):
                m.send(rows, rows, YM[g][3 - 2 * d], at(y=ys[1 + 2 * d]), home[g])
        else:
            guarded(home[g], lambda: m.wait(YM[g][j]))
            if (g, j) in ((0, 3), (1, 1)):
                m.send(rows, rows, YM[g][2], at(y=ys[1 + 2 * g]), home[g])
        guarded(away[g], lambda: m.wait(ZAB[g][j]))
        m.send(rows, rows, ZAB[g][j], cross, home[g])
        m.send(rows, rows, SEC[g][j], at(zl=1 - zl))
        m.send(rows, rows, DIE[g][0][j], at(c=1 - c))

    def j_second(g):
        for j in (0, 3, 1, 2):
            rows = jv.at[g, piece(1 - prim, units[j], c)]
            m.wait(SEC[g][j])
            m.send(rows, rows, DIE[g][1][j], at(c=1 - c))

    def j_finish(g):
        for s in range(2):
            for j in range(4):
                m.wait(DIE[g][s][j])

    R1, R2, R4 = slots(2, 2, 2), slots(2, 2, 4), slots(2, 4)
    put = [pltpu.make_async_copy(nv.at[g, piece(zl, x, c)], out.at[2 * own + g], ls.at[3 + g]) for g in range(2)]

    def n_first(g):
        for kk in range(2):
            for d in range(2):
                k = kk + 2 * d
                m.send(nv.at[g, piece(quad[k][0], xs[2], quad[k][1])], fw.at[g, d, kk], R1[g][d][kk], at(x=xs[1 + 2 * d]))
        for kk in range(2):
            for d in range(2):
                k = kk + 2 - 2 * d
                m.send(nv.at[g, piece(quad[k][0], xs[1 + 2 * d], quad[k][1])], rb.at[g, d, k], R2[g][d][k], at(x=xs[1 + 2 * d]))

    def n_second(g):
        for kk in range(2):
            for d in range(2):
                k = kk + 2 * d
                m.wait(R1[g][d][kk])
                rows = nv.at[g, piece(quad[k][0], xs[1 + 2 * d], quad[k][1])]
                rows[...] += fw[g, d, kk]
                m.send(rows, rb.at[g, d, k], R2[g][d][k], at(x=xs[1 + 2 * d]))

    def n_third(g):
        for k in (2, 3, 1, 0):
            rows = nv.at[g, piece(quad[k][0], x, quad[k][1])]
            m.wait(R2[g][0][k])
            m.wait(R2[g][1][k])
            rows[...] += rb[g, 0, k] + rb[g, 1, k]
            if k == 0:
                put[g].start()
            else:
                m.send(rows, out.at[2 * own + g], R4[g][k], at(zl=quad[k][0], c=quad[k][1]))

    def n_finish(g):
        for k in range(1, 4):
            m.wait(R4[g][k])
        put[g].wait()

    D1, D2, D3, D4, D5 = slots(2, 2, 4), slots(2, 4), slots(2, 4), slots(2, 4), slots(2)
    root_put = pltpu.make_async_copy(fv.at[0, piece(zl, x, c)], extra.at[0], ls.at[5])
    order = (2, 3, 1, 0)

    def f_first(g):
        for s in (1, 0):
            for j in order:
                m.send(fv.at[g, piece(prim if s == 0 else 1 - prim, units[j], 1 - c)], db.at[g, s, j], D1[g][s][j], at(c=1 - c))

    def f_second(g):
        for j in order:
            rows = fv.at[g, piece(1 - prim, units[j], c)]
            m.wait(D1[g][1][j])
            rows[...] += db[g, 1, j]
            m.send(rows, zb.at[g, j], D2[g][j], at(zl=1 - zl))

    def f_third(g):
        for j in order:
            rows = fv.at[g, piece(prim, units[j], c)]
            m.wait(D1[g][0][j])
            m.wait(D2[g][j])
            rows[...] += db[g, 0, j] + zb[g, j]
            m.send(rows, zc.at[g, j], D3[g][j], cross, away[g])

    def f_fourth(g):
        def go():
            for j in order:
                rows = fv.at[g, piece(prim, units[j], c)]
                m.wait(D3[g][j])
                rows[...] += zc[g, j]

        pl.when(home[g])(go)
        via = 3 if g == 0 else 1
        m.send(fv.at[g, piece(prim, units[2], c)], yb.at[g, 2], D4[g][2], at(y=ys[via]), home[g])
        m.send(fv.at[g, piece(prim, units[4 - via], c)], yb.at[g, via], D4[g][via], at(y=ys[4 - via]), home[g])

    def f_fifth(g):
        via = 3 if g == 0 else 1
        rows = fv.at[g, piece(prim, units[via], c)]

        def go():
            m.wait(D4[g][2])
            rows[...] += yb[g, 2]

        pl.when(home[g])(go)
        m.send(rows, yb.at[g, 4 - via], D4[g][4 - via], at(y=ys[via]), home[g])

    def f_sixth(g):
        rows = fv.at[g, piece(prim, units[0], c)]

        def go():
            m.wait(D4[g][1])
            m.wait(D4[g][3])
            rows[...] += yb[g, 1] + yb[g, 3]

        pl.when(home[g])(go)
        if g == 0:
            guarded(at_home_0, root_put.start)
        m.send(rows, extra.at[g], D5[g], source, takes[g])

    def f_finish(g):
        guarded(gives_away[g], lambda: m.wait(D5[g]))
        if g == 0:
            guarded(at_home_0, root_put.wait)

    i_first(0)
    i_spread(0, 0)
    j_first(0)
    i_first(1)
    j_first(1)
    for k in range(1, 4):
        i_spread(0, k)
    j_step(0, 0)
    i_spread(1, 0)
    j_step(0, 3)
    j_step(0, 1)
    i_forward(0)
    j_step(0, 2)
    for k in range(1, 4):
        i_spread(1, k)
    j_second(0)
    for j in (0, 3, 1, 2):
        j_step(1, j)
    i_finish(0)
    j_finish(0)

    def do(*steps):
        def run():
            for step in steps:
                step()

        return run

    plan = {
        (0, 1): do(lambda: i_forward(1), lambda: j_second(1)),
        (1, 0): do(lambda: j_finish(1)),
        (2, 0): do(lambda: n_first(0), lambda: i_finish(1)),
        (2, 2): do(lambda: n_second(0)),
        (3, 0): do(lambda: f_first(1)),
        (3, 1): do(lambda: f_second(1)),
        (3, 2): do(lambda: f_third(1)),
    }

    def point(t, stage):
        for (tt, ss_), run in plan.items():
            if ss_ == stage:
                pl.when(t == tt)(run)

    transform_pairs(iv, jv, nv, fv, a, k_ref, wz_ref, wi_ref, ty_ref, tyi_ref, tx_ref, point)
    n_first(1)
    f_first(0)
    f_fourth(1)
    f_second(0)
    n_second(1)
    n_third(0)
    f_fifth(1)
    f_third(0)
    f_sixth(1)
    n_third(1)
    f_fourth(0)
    f_fifth(0)
    f_sixth(0)
    for g in range(2):
        n_finish(g)
        f_finish(g)
    m.finish()


SENDS, RECEIVES = 256, 256


def run_pairs(own):
    vm = pl.BlockSpec(memory_space=pltpu.VMEM)
    an = pl.BlockSpec(memory_space=pl.ANY)
    f32 = jnp.float32
    big = pltpu.VMEM((2, 6912, 128), f32)

    def pieces(*lead):
        return pltpu.VMEM(lead + (PIECE, 128), f32)

    return pl.pallas_call(
        exchange,
        out_shape=[jax.ShapeDtypeStruct((8, PIECE, 128), f32), jax.ShapeDtypeStruct((2, PIECE, 128), f32)],
        in_specs=[an] + [vm] * 6,
        out_specs=[an, an],
        scratch_shapes=[big] * 4
        + [pltpu.VMEM((96 * 97, 128), f32), pieces(2, 2, 2), pieces(2, 2, 4), pieces(2, 2, 4), pieces(2, 4), pieces(2, 4), pieces(2, 4)]
        + [pltpu.SemaphoreType.DMA((SENDS,)), pltpu.SemaphoreType.DMA((RECEIVES,)), pltpu.SemaphoreType.DMA((8,))],
        compiler_params=pltpu.CompilerParams(vmem_limit_bytes=67043328, collective_id=1, has_side_effects=True),
    )(own, kernel_table(), *tables())


def local(orbitals):
    own = orbitals.reshape(8, PIECE, 128)
    near, far = run_pairs(own)
    gives = lax.axis_index("y") < 2
    out = near.at[0:2].add(jnp.where(gives, far, 0.0))
    return out.reshape(8, 6, 9216)


def solution(mesh):
    fine = jax.sharding.Mesh(mesh.devices.reshape(4, 2, 2, 4, 2), ("y", "zh", "zl", "x", "c"))
    placed = P(("y", "zh"), ("zl", "x", "c"), None)
    return jax.shard_map(local, mesh=fine, in_specs=(placed,), out_specs=placed, check_vma=False)
```

time: 279 us -> 222 us (0.80); the launches traced: 274 us -> 220 us
  Pallas kernels: 258 us -> 205 us
    pallas_call x1, Pallas kernels: 258 us -> 205 us  [run_pairs(): pl.pallas_call(exchange, out_shape=[jax.ShapeDtypeStruct((8, PIECE, 128),...]
where the time goes in v3:
time: 222 us; the launch traced here: 220 us
  Pallas kernels  205 us (92%)
  local copies, waits for them, and re-layouts  8.39 us (4%)
  other arithmetic  7.12 us (3%)
    pallas_call x1, Pallas kernels, run_pairs(): pl.pallas_call(exchange, out_shape=[jax.ShapeDtypeStruct((8, PIECE, 128),...  205 us
    mul x1, other arithmetic, kernel_table(): return (val * (-0.25 / float(N ** 3))).reshape(N * N, 128)  5.13 us

profile of v3, /device:TPU:8, one launch (start us, length us, event | category | flops | bytes accessed | tf_op | source)
XLA Modules:
  0.0 220.2 jit_solution(11852979194254530783)
XLA Ops:
  0.0 2.5 %copy.9 = f32[8,6,9216]{2,1,0:T(8,128)S(1)} copy(f32[8,6,9216]{2,0,1:T(8,128)} %param.8) | data formatting | bytes 3538944 | tf_op args[0]
  2.5 1.6 reshape.90.o
  4.2 0.1 add.54
  4.2 0.1 add.55
  4.4 0.1 add.57
  4.5 5.1 %fusion.k_ref = f32[9216,128]{1,0:T(8,128)} fusion(f32[128]{0:T(128)S(1)} %pad.6, f32[9216]{0:T(1024)S(1)} %add.58), kind=kLoop, calls=%fused_computation.2 | loop fusion | flops 12976128 | bytes 4755968 | tf_op jit(solution)/shard_map/mul | solution.py:57
  9.6 204.7 %shard_map.64 = (f32[8,432,128]{2,1,0:T(8,128)}, f32[2,432,128]{2,1,0:T(8,128)}) custom-call(f32[8,432,128]{2,1,0:T(8,128)} %reshape.90.o, f32[9216,128]{1,0:T(8,128)} %fusion.k_ref, bf16[4,256,256]{2,1,0:T(8,128)(2,1)} %constant.68.clone.wz_ref, bf16[4,256,256]{2,1,0:T(8,128)(2,1)} %constant.69.clone.wi_ref, bf16[192,192]{1,0:T(8,128)(2,1)} %constant.70.clone.ty_ref, ...), custom_call_target="tpu_custom_call" | custom-call | tf_op jit(solution)/shard_map/pallas_call | solution.py:475
  214.3 2.0 add_dynamic-update-slice_fusion
  216.3 1.7 reshape.91
  218.0 2.2 %copy.10 = f32[8,6,9216]{2,0,1:T(8,128)} copy(f32[8,6,9216]{2,1,0:T(8,128)S(1)} %reshape.91) | data formatting | bytes 3538944 | tf_op jit(solution)/shard_map/reshape | solution.py:492
  (4 shorter events, 0.1 us)

commit v4 on v3

--- a/solution.py
+++ b/solution.py
@@ -181,7 +181,7 @@
     return pl.ds(pl.multiple_of((zl * 8 + x * 2 + c) * PIECE, PIECE), PIECE)
 
 
-def exchange(o, k_ref, wz_ref, wi_ref, ty_ref, tyi_ref, tx_ref, out, extra, iv, jv, nv, fv, a, fw, rb, db, zb, zc, yb, ss, rs, ls):
+def exchange(o, k_ref, wz_ref, wi_ref, ty_ref, tyi_ref, tx_ref, out, extra, iv, jv, nv, fv, a, fw, rb, db, zb, yb, ss, rs, ls):
     y, zh, zl, x, c = (lax.axis_index(n) for n in ("y", "zh", "zl", "x", "c"))
     xs = [lax.rem(x + d, 4) for d in range(4)]
     ys = [lax.rem(y + d, 4) for d in range(4)]
@@ -210,7 +210,8 @@
 
     barrier = pltpu.get_barrier_semaphore()
     cross = at(zh=1 - zh, zl=1 - zl)
-    friends = [at(x=xs[1]), at(x=xs[2]), at(x=xs[3]), at(y=ys[1]), at(y=ys[3]), cross]
+    opposite = at(zh=1 - zh)
+    friends = [at(x=xs[d]) for d in range(1, 4)] + [at(y=ys[d]) for d in range(1, 4)] + [cross, opposite]
     friends += [at(zl=qz, c=qc) for qz, qc in quad[1:]]
     for f in friends:
         pl.semaphore_signal(barrier, inc=1, device_id=f, device_id_type=MESH)
@@ -226,7 +227,8 @@
         return [slots(*shape[1:]) for _ in range(shape[0])] if shape else m.slot()
 
     S1, S2, S3 = slots(2, 4), slots(2, 2, 4), slots(2, 2, 2)
-    J1, YM, ZAB, SEC, DIE = slots(2), slots(2, 4), slots(2, 4), slots(2, 4), slots(2, 2, 4)
+    J1, ZP, ZS, YR, DIE = slots(2), slots(2), slots(2), slots(2, 2, 4), slots(2, 2, 4)
+    kind = [prim, 1 - prim]
     keep = [pltpu.make_async_copy(o.at[2 * own + g], iv.at[g, piece(zl, x, c)], ls.at[g]) for g in range(2)]
     root_keep = pltpu.make_async_copy(o.at[0], jv.at[0, piece(zl, x, c)], ls.at[2])
 
@@ -266,28 +268,33 @@
         if g == 0:
             guarded(at_home_0, root_keep.start)
 
-    def j_step(g, j):
-        rows = jv.at[g, piece(prim, units[j], c)]
-        if j == 0:
-            if g == 0:
-                guarded(at_home_0, root_keep.wait)
-            guarded(takes[g], lambda: m.wait(J1[g]))
-            for d in range(2):
-                m.send(rows, rows, YM[g][3 - 2 * d], at(y=ys[1 + 2 * d]), home[g])
-        else:
-            guarded(home[g], lambda: m.wait(YM[g][j]))
-            if (g, j) in ((0, 3), (1, 1)):
-                m.send(rows, rows, YM[g][2], at(y=ys[1 + 2 * g]), home[g])
-        guarded(away[g], lambda: m.wait(ZAB[g][j]))
-        m.send(rows, rows, ZAB[g][j], cross, home[g])
-        m.send(rows, rows, SEC[g][j], at(zl=1 - zl))
-        m.send(rows, rows, DIE[g][0][j], at(c=1 - c))
-
-    def j_second(g):
-        for j in (0, 3, 1, 2):
-            rows = jv.at[g, piece(1 - prim, units[j], c)]
-            m.wait(SEC[g][j])
-            m.send(rows, rows, DIE[g][1][j], at(c=1 - c))
+    def j_row(g, kd):
+        rows = jv.at[g, piece(kind[kd], units[0], c)]
+        for j in (1, 3, 2):
+            m.send(rows, rows, YR[g][kd][4 - j], at(y=ys[j]))
+        m.send(rows, rows, DIE[g][kd][0], at(c=1 - c))
+
+    def j_entry(g):
+        rows = jv.at[g, piece(prim, units[0], c)]
+        if g == 0:
+            guarded(at_home_0, root_keep.wait)
+        guarded(takes[g], lambda: m.wait(J1[g]))
+        m.send(rows, rows, ZP[g], cross, home[g])
+        m.send(rows, rows, ZS[g], at(zl=1 - zl), home[g])
+        m.send(rows, rows, ZS[g], opposite, home[g])
+        guarded(away[g], lambda: m.wait(ZP[g]))
+        j_row(g, 0)
+
+    def j_other(g):
+        m.wait(ZS[g])
+        j_row(g, 1)
+
+    def j_rows(g):
+        for kd in range(2):
+            for j in (3, 1, 2):
+                rows = jv.at[g, piece(kind[kd], units[j], c)]
+                m.wait(YR[g][kd][j])
+                m.send(rows, rows, DIE[g][kd][j], at(c=1 - c))
 
     def j_finish(g):
         for s in range(2):
@@ -332,60 +339,42 @@
             m.wait(R4[g][k])
         put[g].wait()
 
-    D1, D2, D3, D4, D5 = slots(2, 2, 4), slots(2, 4), slots(2, 4), slots(2, 4), slots(2)
+    D1, D2, D3, D5 = slots(2, 2, 4), slots(2, 2, 4), slots(2, 3), slots(2)
     root_put = pltpu.make_async_copy(fv.at[0, piece(zl, x, c)], extra.at[0], ls.at[5])
-    order = (2, 3, 1, 0)
 
     def f_first(g):
-        for s in (1, 0):
-            for j in order:
-                m.send(fv.at[g, piece(prim if s == 0 else 1 - prim, units[j], 1 - c)], db.at[g, s, j], D1[g][s][j], at(c=1 - c))
+        for j in (2, 1, 3, 0):
+            for kd in range(2):
+                m.send(fv.at[g, piece(kind[kd], units[j], 1 - c)], db.at[g, kd, j], D1[g][kd][j], at(c=1 - c))
 
     def f_second(g):
-        for j in order:
-            rows = fv.at[g, piece(1 - prim, units[j], c)]
-            m.wait(D1[g][1][j])
-            rows[...] += db[g, 1, j]
-            m.send(rows, zb.at[g, j], D2[g][j], at(zl=1 - zl))
+        for j in (2, 1, 3, 0):
+            for kd in (1, 0):
+                rows = fv.at[g, piece(kind[kd], units[j], c)]
+                m.wait(D1[g][kd][j])
+                rows[...] += db[g, kd, j]
+                if j:
+                    m.send(rows, yb.at[g, kd, j], D2[g][kd][j], at(y=ys[j]))
 
     def f_third(g):
-        for j in order:
-            rows = fv.at[g, piece(prim, units[j], c)]
-            m.wait(D1[g][0][j])
-            m.wait(D2[g][j])
-            rows[...] += db[g, 0, j] + zb[g, j]
-            m.send(rows, zc.at[g, j], D3[g][j], cross, away[g])
+        for kd in (1, 0):
+            rows = fv.at[g, piece(kind[kd], units[0], c)]
+            for j in (1, 3, 2):
+                m.wait(D2[g][kd][j])
+            rows[...] += (yb[g, kd, 1] + yb[g, kd, 2]) + yb[g, kd, 3]
+            if kd:
+                m.send(rows, zb.at[g, 0], D3[g][0], at(zl=1 - zl), home[g])
+                m.send(rows, zb.at[g, 1], D3[g][1], opposite, away[g])
+            else:
+                m.send(rows, zb.at[g, 2], D3[g][2], cross, away[g])
 
     def f_fourth(g):
+        rows = fv.at[g, piece(prim, units[0], c)]
+
         def go():
-            for j in order:
-                rows = fv.at[g, piece(prim, units[j], c)]
-                m.wait(D3[g][j])
-                rows[...] += zc[g, j]
-
-        pl.when(home[g])(go)
-        via = 3 if g == 0 else 1
-        m.send(fv.at[g, piece(prim, units[2], c)], yb.at[g, 2], D4[g][2], at(y=ys[via]), home[g])
-        m.send(fv.at[g, piece(prim, units[4 - via], c)], yb.at[g, via], D4[g][via], at(y=ys[4 - via]), home[g])
-
-    def f_fifth(g):
-        via = 3 if g == 0 else 1
-        rows = fv.at[g, piece(prim, units[via], c)]
-
-        def go():
-            m.wait(D4[g][2])
-            rows[...] += yb[g, 2]
-
-        pl.when(home[g])(go)
-        m.send(rows, yb.at[g, 4 - via], D4[g][4 - via], at(y=ys[via]), home[g])
-
-    def f_sixth(g):
-        rows = fv.at[g, piece(prim, units[0], c)]
-
-        def go():
-            m.wait(D4[g][1])
-            m.wait(D4[g][3])
-            rows[...] += yb[g, 1] + yb[g, 3]
+            for e in range(3):
+                m.wait(D3[g][e])
+            rows[...] += (zb[g, 0] + zb[g, 1]) + zb[g, 2]
 
         pl.when(home[g])(go)
         if g == 0:
@@ -404,17 +393,15 @@
     j_first(1)
     for k in range(1, 4):
         i_spread(0, k)
-    j_step(0, 0)
+    j_entry(0)
     i_spread(1, 0)
-    j_step(0, 3)
-    j_step(0, 1)
+    j_entry(1)
+    j_other(0)
     i_forward(0)
-    j_step(0, 2)
+    j_other(1)
     for k in range(1, 4):
         i_spread(1, k)
-    j_second(0)
-    for j in (0, 3, 1, 2):
-        j_step(1, j)
+    j_rows(0)
     i_finish(0)
     j_finish(0)
 
@@ -426,13 +413,14 @@
         return run
 
     plan = {
-        (0, 1): do(lambda: i_forward(1), lambda: j_second(1)),
+        (0, 1): do(lambda: j_rows(1)),
+        (0, 2): do(lambda: i_forward(1)),
         (1, 0): do(lambda: j_finish(1)),
         (2, 0): do(lambda: n_first(0), lambda: i_finish(1)),
         (2, 2): do(lambda: n_second(0)),
         (3, 0): do(lambda: f_first(1)),
         (3, 1): do(lambda: f_second(1)),
-        (3, 2): do(lambda: f_third(1)),
+        (3, 2): do(lambda: n_third(0)),
     }
 
     def point(t, stage):
@@ -443,17 +431,13 @@
     transform_pairs(iv, jv, nv, fv, a, k_ref, wz_ref, wi_ref, ty_ref, tyi_ref, tx_ref, point)
     n_first(1)
     f_first(0)
+    f_second(0)
+    f_third(1)
+    n_second(1)
     f_fourth(1)
-    f_second(0)
-    n_second(1)
-    n_third(0)
-    f_fifth(1)
     f_third(0)
-    f_sixth(1)
+    f_fourth(0)
     n_third(1)
-    f_fourth(0)
-    f_fifth(0)
-    f_sixth(0)
     for g in range(2):
         n_finish(g)
         f_finish(g)
@@ -478,7 +462,7 @@
         in_specs=[an] + [vm] * 6,
         out_specs=[an, an],
         scratch_shapes=[big] * 4
-        + [pltpu.VMEM((96 * 97, 128), f32), pieces(2, 2, 2), pieces(2, 2, 4), pieces(2, 2, 4), pieces(2, 4), pieces(2, 4), pieces(2, 4)]
+        + [pltpu.VMEM((96 * 97, 128), f32), pieces(2, 2, 2), pieces(2, 2, 4), pieces(2, 2, 4), pieces(2, 3), pieces(2, 2, 4)]
         + [pltpu.SemaphoreType.DMA((SENDS,)), pltpu.SemaphoreType.DMA((RECEIVES,)), pltpu.SemaphoreType.DMA((8,))],
         compiler_params=pltpu.CompilerParams(vmem_limit_bytes=67043328, collective_id=1, has_side_effects=True),
     )(own, kernel_table(), *tables())

time: 222 us -> 201 us (0.905)
  Pallas kernels: 205 us -> 184 us
    pallas_call x1, Pallas kernels: 205 us -> 184 us  [run_pairs(): pl.pallas_call(exchange, out_shape=[jax.ShapeDtypeStruct((8, PIECE, 128),...]
where the time goes in v4:
time: 201 us; the launch traced here: 200 us
  Pallas kernels  184 us (92%)
  local copies, waits for them, and re-layouts  8.39 us (4%)
  other arithmetic  7.12 us (4%)
    pallas_call x1, Pallas kernels, run_pairs(): pl.pallas_call(exchange, out_shape=[jax.ShapeDtypeStruct((8, PIECE, 128),...  184 us
    mul x1, other arithmetic, kernel_table(): return (val * (-0.25 / float(N ** 3))).reshape(N * N, 128)  5.13 us

profile of v4, /device:TPU:8, one launch (start us, length us, event | category | flops | bytes accessed | tf_op | source)
XLA Modules:
  0.0 199.9 jit_solution(12849810308977783054)
XLA Ops:
  0.0 2.5 %copy.9 = f32[8,6,9216]{2,1,0:T(8,128)S(1)} copy(f32[8,6,9216]{2,0,1:T(8,128)} %param.8) | data formatting | bytes 3538944 | tf_op args[0]
  2.5 1.6 reshape.90.o
  4.2 0.1 add.54
  4.2 0.1 add.55
  4.4 0.1 add.57
  4.5 5.1 %fusion.k_ref = f32[9216,128]{1,0:T(8,128)} fusion(f32[128]{0:T(128)S(1)} %pad.6, f32[9216]{0:T(1024)S(1)} %add.58), kind=kLoop, calls=%fused_computation.2 | loop fusion | flops 12976128 | bytes 4755968 | tf_op jit(solution)/shard_map/mul | solution.py:57
  9.6 184.4 %shard_map.64 = (f32[8,432,128]{2,1,0:T(8,128)}, f32[2,432,128]{2,1,0:T(8,128)}) custom-call(f32[8,432,128]{2,1,0:T(8,128)} %reshape.90.o, f32[9216,128]{1,0:T(8,128)} %fusion.k_ref, bf16[4,256,256]{2,1,0:T(8,128)(2,1)} %constant.68.clone.wz_ref, bf16[4,256,256]{2,1,0:T(8,128)(2,1)} %constant.69.clone.wi_ref, bf16[192,192]{1,0:T(8,128)(2,1)} %constant.70.clone.ty_ref, ...), custom_call_target="tpu_custom_call" | custom-call | tf_op jit(solution)/shard_map/pallas_call | solution.py:459
  194.0 2.0 add_dynamic-update-slice_fusion
  196.0 1.7 reshape.91
  197.7 2.2 %copy.10 = f32[8,6,9216]{2,0,1:T(8,128)} copy(f32[8,6,9216]{2,1,0:T(8,128)S(1)} %reshape.91) | data formatting | bytes 3538944 | tf_op jit(solution)/shard_map/reshape | solution.py:476
  (4 shorter events, 0.1 us)

commit v5 on v4

--- a/solution.py
+++ b/solution.py
@@ -44,17 +44,28 @@
     tx = two(hi, lo)
     return wz, wi, ty, tyi, tx
 
-def kernel_table():
-    idx = jnp.arange(N, dtype=jnp.int32)
-    f = jnp.where(idx <= N//2, idx, idx-N).astype(jnp.float32)
-    sq = f*f
-    sqw = jnp.pad(sq, (0,32))
-    g2 = (2.0*math.pi/CELL)**2 * (sq[:,None,None]+sq[None,:,None]+sqw[None,None,:])
-    pos = g2 > 0
-    safe = jnp.where(pos, g2, 1.0)
-    val = 4.0*math.pi/safe * -jnp.expm1(-safe/(4.0*OMEGA*OMEGA))
-    val = jnp.where(pos, val, math.pi/(OMEGA*OMEGA))
-    return (val * (-0.25/float(N**3))).reshape(N*N, 128)
+def build_kernel(k_ref):
+    def square(index):
+        index = index.astype(jnp.float32)
+        freq = jnp.where(index <= N // 2, index, index - N)
+        return freq * freq
+
+    u = square(lax.broadcasted_iota(jnp.int32, (N, 128), 0))
+    w = square(jnp.minimum(lax.broadcasted_iota(jnp.int32, (N, 128), 1), N - 1))
+    plane = u + w
+    scale = (2.0 * math.pi / CELL) ** 2
+    factor = -0.25 / float(N**3)
+
+    def one(v, _):
+        g_two = scale * (plane + square(v))
+        positive = g_two > 0
+        safe = jnp.where(positive, g_two, 1.0)
+        value = (4.0 * math.pi * factor) / safe * (1.0 - jnp.exp(safe * (-1.0 / (4.0 * OMEGA * OMEGA))))
+        k_ref[pl.ds(pl.multiple_of(v * N, 8), N), :] = jnp.where(positive, value, math.pi / (OMEGA * OMEGA) * factor)
+        return 0
+
+    lax.fori_loop(0, N, one, 0)
+
 
 def split(x):
     hi = x.astype(bf)
@@ -181,7 +192,10 @@
     return pl.ds(pl.multiple_of((zl * 8 + x * 2 + c) * PIECE, PIECE), PIECE)
 
 
-def exchange(o, k_ref, wz_ref, wi_ref, ty_ref, tyi_ref, tx_ref, out, extra, iv, jv, nv, fv, a, fw, rb, db, zb, yb, ss, rs, ls):
+def exchange(orbitals, wz_ref, wi_ref, ty_ref, tyi_ref, tx_ref, action, k_ref, planes, o, out, extra, hb, iv, jv, nv, fv, a, fw, rb, db, zb, yb, ss, rs, ls):
+    fetch = [pltpu.make_async_copy(orbitals.at[b], planes.at[b], ls.at[8 + b]) for b in range(6)]
+    for copy in fetch:
+        copy.start()
     y, zh, zl, x, c = (lax.axis_index(n) for n in ("y", "zh", "zl", "x", "c"))
     xs = [lax.rem(x + d, 4) for d in range(4)]
     ys = [lax.rem(y + d, 4) for d in range(4)]
@@ -201,12 +215,25 @@
     def at(y=y, zh=zh, zl=zl, x=x, c=c):
         return (y, zh, zl, x, c)
 
-    entry = [at(x=lax.rem(band, 4), y=lax.rem(y + shift, 4)), at(x=lax.rem(band, 4), y=lax.rem(y + shift, 4), zh=1 - zh, zl=1 - zl)]
+    relay = [at(y=lax.rem(y + shift, 4)), at(y=lax.rem(y + shift, 4), zh=1 - zh, zl=1 - zl)]
     source = at(x=units[0], y=root_y, zh=root_zh, zl=prim)
     at_home_0 = jnp.logical_and(in_root_zh, dy == 0)
     gives_away = [jnp.logical_and(gives, shift != 0), gives]
+    diagonal = lax.rem(x + 4 - y, 4)
+    is_relay, passes, passed_to, passed_from = [], [], [], []
+    for g in range(2):
+        zr = zh if g == 0 else 1 - zh
+        second = jnp.where(diagonal == zr, 0, 1)
+        target = zr + 2 * second
+        on_path = jnp.logical_or(diagonal == zr, diagonal == zr + 1)
+        moves = jnp.logical_and(on_path, x != target)
+        is_relay.append(moves if g == 0 else on_path)
+        passes.append(moves)
+        passed_to.append(at(x=target))
+        passed_from.append(at(y=second, zh=zr, zl=zl if g == 0 else 1 - zl))
+    stays = jnp.logical_and(is_relay[1], jnp.logical_not(passes[1]))
     takes = [jnp.logical_and(in_root_zh, dy != 0), home[1]]
-    gets = jnp.logical_not(at_home_0)
+    arrives = [takes[0], jnp.logical_and(takes[1], dy != 0)]
 
     barrier = pltpu.get_barrier_semaphore()
     cross = at(zh=1 - zh, zl=1 - zl)
@@ -216,33 +243,46 @@
     for f in friends:
         pl.semaphore_signal(barrier, inc=1, device_id=f, device_id_type=MESH)
     for g in range(2):
-        guarded(gives_away[g], lambda: pl.semaphore_signal(barrier, inc=1, device_id=entry[g], device_id_type=MESH))
-    guarded(gets, lambda: pl.semaphore_signal(barrier, inc=1, device_id=source, device_id_type=MESH))
-    count = gets.astype(jnp.int32) + gives_away[0].astype(jnp.int32) + gives_away[1].astype(jnp.int32)
+        guarded(gives_away[g], lambda: pl.semaphore_signal(barrier, inc=1, device_id=relay[g], device_id_type=MESH))
+        guarded(is_relay[g], lambda: pl.semaphore_signal(barrier, inc=1, device_id=passed_from[g], device_id_type=MESH))
+    count = sum(flag.astype(jnp.int32) for flag in gives_away + is_relay)
+    for copy in fetch:
+        copy.wait()
+
+    def unpack(b, _):
+        for q in range(72):
+            o[pl.ds(b * 72 + q, 8, stride=PIECE), :] = planes[b, :, 128 * q:128 * q + 128]
+        return 0
+
+    lax.fori_loop(0, 6, unpack, 0)
     pl.semaphore_wait(barrier, len(friends) + count)
 
     m = Comm(ss, rs, fw.at[0, 0, 0])
+
+    def orbital(ref, b):
+        return ref.at[pl.ds(pl.multiple_of(b * PIECE, PIECE), PIECE)]
+
 
     def slots(*shape):
         return [slots(*shape[1:]) for _ in range(shape[0])] if shape else m.slot()
 
     S1, S2, S3 = slots(2, 4), slots(2, 2, 4), slots(2, 2, 2)
-    J1, ZP, ZS, YR, DIE = slots(2), slots(2), slots(2), slots(2, 2, 4), slots(2, 2, 4)
+    JA, J1, ZP, ZS, YR, DIE = slots(2), slots(2), slots(2), slots(2), slots(2, 2, 4), slots(2, 2, 4)
     kind = [prim, 1 - prim]
-    keep = [pltpu.make_async_copy(o.at[2 * own + g], iv.at[g, piece(zl, x, c)], ls.at[g]) for g in range(2)]
-    root_keep = pltpu.make_async_copy(o.at[0], jv.at[0, piece(zl, x, c)], ls.at[2])
+    keep = [pltpu.make_async_copy(orbital(o, 2 * own + g), iv.at[g, piece(zl, x, c)], ls.at[g]) for g in range(2)]
+    root_keep = pltpu.make_async_copy(orbital(o, 0), jv.at[0, piece(zl, x, c)], ls.at[2])
 
     def i_first(g):
         for k in range(1, 4):
             qz, qc = quad[k]
-            m.send(o.at[2 * (2 * qz + qc) + g], iv.at[g, piece(zl, x, c)], S1[g][k], at(zl=qz, c=qc))
+            m.send(orbital(o, 2 * (2 * qz + qc) + g), iv.at[g, piece(zl, x, c)], S1[g][k], at(zl=qz, c=qc))
         keep[g].start()
 
     def i_spread(g, k):
         rows = piece(quad[k][0], x, quad[k][1])
         src = iv.at[g, rows]
         if k == 0:
-            src = o.at[2 * own + g]
+            src = orbital(o, 2 * own + g)
         else:
             m.wait(S1[g][k])
         for d in range(2):
@@ -263,10 +303,18 @@
                 m.wait(S2[g][d][kk + 2 - 2 * d])
                 m.wait(S3[g][d][kk])
 
+    stay = pltpu.make_async_copy(hb.at[0, 1], jv.at[1, piece(prim, units[0], c)], ls.at[6])
+
     def j_first(g):
-        m.send(o.at[g], jv.at[g, piece(zl, x, c)], J1[g], entry[g], gives_away[g])
+        m.send(orbital(o, g), hb.at[0, g], JA[g], relay[g], gives_away[g])
         if g == 0:
             guarded(at_home_0, root_keep.start)
+
+    def j_relay(g):
+        guarded(is_relay[g], lambda: m.wait(JA[g]))
+        m.send(hb.at[0, g], jv.at[g, piece(zl if g == 0 else 1 - zl, x, c)], J1[g], passed_to[g], passes[g])
+        if g == 1:
+            guarded(stays, stay.start)
 
     def j_row(g, kd):
         rows = jv.at[g, piece(kind[kd], units[0], c)]
@@ -278,7 +326,9 @@
         rows = jv.at[g, piece(prim, units[0], c)]
         if g == 0:
             guarded(at_home_0, root_keep.wait)
-        guarded(takes[g], lambda: m.wait(J1[g]))
+        else:
+            guarded(stays, stay.wait)
+        guarded(arrives[g], lambda: m.wait(J1[g]))
         m.send(rows, rows, ZP[g], cross, home[g])
         m.send(rows, rows, ZS[g], at(zl=1 - zl), home[g])
         m.send(rows, rows, ZS[g], opposite, home[g])
@@ -302,7 +352,7 @@
                 m.wait(DIE[g][s][j])
 
     R1, R2, R4 = slots(2, 2, 2), slots(2, 2, 4), slots(2, 4)
-    put = [pltpu.make_async_copy(nv.at[g, piece(zl, x, c)], out.at[2 * own + g], ls.at[3 + g]) for g in range(2)]
+    put = [pltpu.make_async_copy(nv.at[g, piece(zl, x, c)], orbital(out, 2 * own + g), ls.at[3 + g]) for g in range(2)]
 
     def n_first(g):
         for kk in range(2):
@@ -332,14 +382,14 @@
             if k == 0:
                 put[g].start()
             else:
-                m.send(rows, out.at[2 * own + g], R4[g][k], at(zl=quad[k][0], c=quad[k][1]))
+                m.send(rows, orbital(out, 2 * own + g), R4[g][k], at(zl=quad[k][0], c=quad[k][1]))
 
     def n_finish(g):
         for k in range(1, 4):
             m.wait(R4[g][k])
         put[g].wait()
 
-    D1, D2, D3, D5 = slots(2, 2, 4), slots(2, 2, 4), slots(2, 3), slots(2)
+    D1, D2, D3, D5, D6 = slots(2, 2, 4), slots(2, 2, 4), slots(2, 3), slots(2), slots(2)
     root_put = pltpu.make_async_copy(fv.at[0, piece(zl, x, c)], extra.at[0], ls.at[5])
 
     def f_first(g):
@@ -379,20 +429,29 @@
         pl.when(home[g])(go)
         if g == 0:
             guarded(at_home_0, root_put.start)
-        m.send(rows, extra.at[g], D5[g], source, takes[g])
+        m.send(rows, hb.at[1, g], D5[g], at(x=units[0]), arrives[g])
+        if g == 1:
+            m.send(rows, extra.at[g], D6[g], source, stays)
+
+    def f_fifth(g):
+        guarded(passes[g], lambda: m.wait(D5[g]))
+        m.send(hb.at[1, g], extra.at[g], D6[g], passed_from[g], passes[g])
 
     def f_finish(g):
-        guarded(gives_away[g], lambda: m.wait(D5[g]))
+        guarded(gives_away[g], lambda: m.wait(D6[g]))
         if g == 0:
             guarded(at_home_0, root_put.wait)
 
+    j_first(0)
     i_first(0)
     i_spread(0, 0)
-    j_first(0)
+    j_first(1)
     i_first(1)
-    j_first(1)
+    build_kernel(k_ref)
     for k in range(1, 4):
         i_spread(0, k)
+    j_relay(0)
+    j_relay(1)
     j_entry(0)
     i_spread(1, 0)
     j_entry(1)
@@ -436,18 +495,39 @@
     n_second(1)
     f_fourth(1)
     f_third(0)
+    f_fifth(1)
     f_fourth(0)
     n_third(1)
+    f_fifth(0)
     for g in range(2):
         n_finish(g)
         f_finish(g)
+
+    for g in range(2):
+
+        def add():
+            out[pl.ds(g * PIECE, PIECE), :] += extra[g]
+
+        pl.when(gives)(add)
+
+    def pack(b, _):
+        for q in range(72):
+            planes[b, :, 128 * q:128 * q + 128] = out[pl.ds(b * 72 + q, 8, stride=PIECE), :]
+        return 0
+
+    lax.fori_loop(0, 6, pack, 0)
+    stores = [pltpu.make_async_copy(planes.at[b], action.at[b], ls.at[8 + b]) for b in range(6)]
+    for store in stores:
+        store.start()
     m.finish()
+    for store in stores:
+        store.wait()
 
 
 SENDS, RECEIVES = 256, 256
 
 
-def run_pairs(own):
+def local(orbitals):
     vm = pl.BlockSpec(memory_space=pltpu.VMEM)
     an = pl.BlockSpec(memory_space=pl.ANY)
     f32 = jnp.float32
@@ -458,22 +538,15 @@
 
     return pl.pallas_call(
         exchange,
-        out_shape=[jax.ShapeDtypeStruct((8, PIECE, 128), f32), jax.ShapeDtypeStruct((2, PIECE, 128), f32)],
-        in_specs=[an] + [vm] * 6,
-        out_specs=[an, an],
-        scratch_shapes=[big] * 4
-        + [pltpu.VMEM((96 * 97, 128), f32), pieces(2, 2, 2), pieces(2, 2, 4), pieces(2, 2, 4), pieces(2, 3), pieces(2, 2, 4)]
-        + [pltpu.SemaphoreType.DMA((SENDS,)), pltpu.SemaphoreType.DMA((RECEIVES,)), pltpu.SemaphoreType.DMA((8,))],
+        out_shape=jax.ShapeDtypeStruct((6, 8, 9216), f32),
+        in_specs=[an] + [vm] * 5,
+        out_specs=an,
+        scratch_shapes=[pltpu.VMEM((N * N, 128), f32), pltpu.VMEM((6, 8, 9216), f32), pltpu.VMEM((8 * PIECE, 128), f32), pltpu.VMEM((8 * PIECE, 128), f32), pieces(2), pieces(2, 2)]
+        + [big] * 4
+        + [pltpu.VMEM((96 * AS, 128), f32), pieces(2, 2, 2), pieces(2, 2, 4), pieces(2, 2, 4), pieces(2, 3), pieces(2, 2, 4)]
+        + [pltpu.SemaphoreType.DMA((SENDS,)), pltpu.SemaphoreType.DMA((RECEIVES,)), pltpu.SemaphoreType.DMA((16,))],
         compiler_params=pltpu.CompilerParams(vmem_limit_bytes=67043328, collective_id=1, has_side_effects=True),
-    )(own, kernel_table(), *tables())
-
-
-def local(orbitals):
-    own = orbitals.reshape(8, PIECE, 128)
-    near, far = run_pairs(own)
-    gives = lax.axis_index("y") < 2
-    out = near.at[0:2].add(jnp.where(gives, far, 0.0))
-    return out.reshape(8, 6, 9216)
+    )(orbitals.transpose(1, 0, 2), *tables()).transpose(1, 0, 2)
 
 
 def solution(mesh):

time: 201 us -> 182 us (0.905)
  other arithmetic: 7.12 us -> 0 us
  local copies, waits for them, and re-layouts: 8.39 us -> 2.8 us
  Pallas kernels: 184 us -> 179 us
    reshape x3 -> x0, local copies, waits for them, and re-layouts: 5.54 us -> none  [the longest x2 3.93 us: local(): return out.reshape(8, 6, 9216)]
    pallas_call x1, Pallas kernels: 184 us -> 179 us  [local(): pl.pallas_call(exchange, out_shape=jax.ShapeDtypeStruct((6, 8, 9216), f32...]
    mul x2 -> x0, other arithmetic: 5.13 us -> none  [the longest x1 5.13 us: kernel_table(): return (val * (-0.25 / float(N ** 3))).reshape(N * N, 128)]
where the time goes in v5:
time: 182 us
  Pallas kernels  179 us (98%)
  local copies, waits for them, and re-layouts  2.8 us (2%)
    pallas_call x1, Pallas kernels, local(): pl.pallas_call(exchange, out_shape=jax.ShapeDtypeStruct((6, 8, 9216), f32...  179 us

profile of v5, /device:TPU:8, one launch (start us, length us, event | category | flops | bytes accessed | tf_op | source)
XLA Modules:
  0.0 181.8 jit_solution(16110099188821423949)
XLA Ops:
  0.0 179.0 %shard_map.64 = f32[6,8,9216]{2,1,0:T(8,128)} custom-call(f32[6,8,9216]{2,1,0:T(8,128)} %bitcast.3, bf16[4,256,256]{2,1,0:T(8,128)(2,1)} %constant.10.clone.wz_ref, bf16[4,256,256]{2,1,0:T(8,128)(2,1)} %constant.11.clone.wi_ref, bf16[192,192]{1,0:T(8,128)(2,1)} %constant.12.clone.ty_ref, bf16[192,192]{1,0:T(8,128)(2,1)} %constant.13.clone.tyi_ref, ...), custom_call_target="tpu_custom_call" | custom-call | tf_op jit(solution)/shard_map/pallas_call | solution.py:539
  179.0 2.8 %copy.8 = f32[8,6,9216]{2,0,1:T(8,128)} copy(f32[8,6,9216]{2,0,1:T(8,128)} %bitcast.2) | data formatting | bytes 3538944

commit v6 on v5

--- a/solution.py
+++ b/solution.py
@@ -156,6 +156,8 @@
 
 MESH = pl.DeviceIdType.MESH
 PIECE = 432
+CHUNKS = 2
+PART = PIECE // CHUNKS
 
 
 class Comm:
@@ -170,15 +172,19 @@
         copy = pltpu.make_async_remote_copy(src_ref=src, dst_ref=dst, send_sem=self.ss.at[self.n], recv_sem=self.rs.at[recv],
                                             device_id=device, device_id_type=MESH)
         self.n += 1
-        self.sent.append(when)
+        self.sent.append((when, src.shape[0]))
         guarded(when, copy.start)
 
-    def wait(self, recv):
-        pltpu.make_async_copy(self.some, self.some, self.rs.at[recv]).wait()
+    def done(self, sem, rows):
+        ref = self.some.at[pl.ds(0, rows)]
+        pltpu.make_async_copy(ref, ref, sem).wait()
+
+    def wait(self, recv, rows=PIECE):
+        self.done(self.rs.at[recv], rows)
 
     def finish(self):
-        for n, when in enumerate(self.sent):
-            guarded(when, pltpu.make_async_copy(self.some, self.some, self.ss.at[n]).wait)
+        for n, (when, rows) in enumerate(self.sent):
+            guarded(when, functools.partial(self.done, self.ss.at[n], rows))
 
 
 def guarded(when, do):
@@ -190,6 +196,10 @@
 
 def piece(zl, x, c):
     return pl.ds(pl.multiple_of((zl * 8 + x * 2 + c) * PIECE, PIECE), PIECE)
+
+
+def chunk(zl, x, c, h):
+    return pl.ds(pl.multiple_of((zl * 8 + x * 2 + c) * PIECE + h * PART, 8), PART)
 
 
 def exchange(orbitals, wz_ref, wi_ref, ty_ref, tyi_ref, tx_ref, action, k_ref, planes, o, out, extra, hb, iv, jv, nv, fv, a, fw, rb, db, zb, yb, ss, rs, ls):
@@ -267,7 +277,8 @@
         return [slots(*shape[1:]) for _ in range(shape[0])] if shape else m.slot()
 
     S1, S2, S3 = slots(2, 4), slots(2, 2, 4), slots(2, 2, 2)
-    JA, J1, ZP, ZS, YR, DIE = slots(2), slots(2), slots(2), slots(2), slots(2, 2, 4), slots(2, 2, 4)
+    JA, J1, ZP, ZS = (slots(2, CHUNKS) for _ in range(4))
+    YR, DIE = (slots(2, CHUNKS, 2, 4) for _ in range(2))
     kind = [prim, 1 - prim]
     keep = [pltpu.make_async_copy(orbital(o, 2 * own + g), iv.at[g, piece(zl, x, c)], ls.at[g]) for g in range(2)]
     root_keep = pltpu.make_async_copy(orbital(o, 0), jv.at[0, piece(zl, x, c)], ls.at[2])
@@ -303,71 +314,89 @@
                 m.wait(S2[g][d][kk + 2 - 2 * d])
                 m.wait(S3[g][d][kk])
 
-    stay = pltpu.make_async_copy(hb.at[0, 1], jv.at[1, piece(prim, units[0], c)], ls.at[6])
+    stay = [pltpu.make_async_copy(hb.at[0, 1, h], jv.at[1, chunk(prim, units[0], c, h)], ls.at[6 + h]) for h in range(2)]
 
     def j_first(g):
-        m.send(orbital(o, g), hb.at[0, g], JA[g], relay[g], gives_away[g])
+        for h in range(CHUNKS):
+            m.send(orbital(o, g).at[pl.ds(h * PART, PART)], hb.at[0, g, h], JA[g][h], relay[g], gives_away[g])
         if g == 0:
             guarded(at_home_0, root_keep.start)
 
-    def j_relay(g):
-        guarded(is_relay[g], lambda: m.wait(JA[g]))
-        m.send(hb.at[0, g], jv.at[g, piece(zl if g == 0 else 1 - zl, x, c)], J1[g], passed_to[g], passes[g])
+    def j_relay(g, h):
+        guarded(is_relay[g], lambda: m.wait(JA[g][h], PART))
+        m.send(hb.at[0, g, h], jv.at[g, chunk(zl if g == 0 else 1 - zl, x, c, h)], J1[g][h], passed_to[g], passes[g])
         if g == 1:
-            guarded(stays, stay.start)
-
-    def j_row(g, kd):
-        rows = jv.at[g, piece(kind[kd], units[0], c)]
-        for j in (1, 3, 2):
-            m.send(rows, rows, YR[g][kd][4 - j], at(y=ys[j]))
-        m.send(rows, rows, DIE[g][kd][0], at(c=1 - c))
-
-    def j_entry(g):
-        rows = jv.at[g, piece(prim, units[0], c)]
+            guarded(stays, stay[h].start)
+
+    def j_row(g, kd, h):
+        rows = jv.at[g, chunk(kind[kd], units[0], c, h)]
+        for j in (1, 3):
+            m.send(rows, rows, YR[g][h][kd][4 - j], at(y=ys[j]))
+        m.send(rows, rows, DIE[g][h][kd][0], at(c=1 - c))
+
+    def j_entry(g, h):
+        rows = jv.at[g, chunk(prim, units[0], c, h)]
         if g == 0:
-            guarded(at_home_0, root_keep.wait)
+            if h == 0:
+                guarded(at_home_0, root_keep.wait)
         else:
-            guarded(stays, stay.wait)
-        guarded(arrives[g], lambda: m.wait(J1[g]))
-        m.send(rows, rows, ZP[g], cross, home[g])
-        m.send(rows, rows, ZS[g], at(zl=1 - zl), home[g])
-        m.send(rows, rows, ZS[g], opposite, home[g])
-        guarded(away[g], lambda: m.wait(ZP[g]))
-        j_row(g, 0)
-
-    def j_other(g):
-        m.wait(ZS[g])
-        j_row(g, 1)
+            guarded(stays, stay[h].wait)
+        guarded(arrives[g], lambda: m.wait(J1[g][h], PART))
+        m.send(rows, rows, ZP[g][h], cross, home[g])
+        m.send(rows, rows, ZS[g][h], at(zl=1 - zl), home[g])
+        m.send(rows, rows, ZS[g][h], opposite, home[g])
+        guarded(away[g], lambda: m.wait(ZP[g][h], PART))
+        j_row(g, 0, h)
+
+    def j_other(g, h):
+        m.wait(ZS[g][h], PART)
+        j_row(g, 1, h)
+
+    def j_take(g, h, kd, j, onward=None):
+        rows = jv.at[g, chunk(kind[kd], units[j], c, h)]
+        m.wait(YR[g][h][kd][j], PART)
+        if onward:
+            m.send(rows, rows, YR[g][h][kd][2], at(y=ys[onward]))
+        m.send(rows, rows, DIE[g][h][kd][j], at(c=1 - c))
+
+    def j_pass(g):
+        for kd in range(2):
+            j_take(g, 0, kd, 3, 1)
+            j_take(g, 1, kd, 1, 3)
 
     def j_rows(g):
         for kd in range(2):
-            for j in (3, 1, 2):
-                rows = jv.at[g, piece(kind[kd], units[j], c)]
-                m.wait(YR[g][kd][j])
-                m.send(rows, rows, DIE[g][kd][j], at(c=1 - c))
+            j_take(g, 0, kd, 1)
+            j_take(g, 1, kd, 3)
+        for kd in range(2):
+            for h in range(CHUNKS):
+                j_take(g, h, kd, 2)
 
     def j_finish(g):
-        for s in range(2):
-            for j in range(4):
-                m.wait(DIE[g][s][j])
+        for h in range(CHUNKS):
+            for kd in range(2):
+                for j in range(4):
+                    m.wait(DIE[g][h][kd][j], PART)
 
     R1, R2, R4 = slots(2, 2, 2), slots(2, 2, 4), slots(2, 4)
     put = [pltpu.make_async_copy(nv.at[g, piece(zl, x, c)], orbital(out, 2 * own + g), ls.at[3 + g]) for g in range(2)]
+
+    through = ((2, 0), (3, 1))
 
     def n_first(g):
         for kk in range(2):
             for d in range(2):
-                k = kk + 2 * d
+                k = through[d][kk]
                 m.send(nv.at[g, piece(quad[k][0], xs[2], quad[k][1])], fw.at[g, d, kk], R1[g][d][kk], at(x=xs[1 + 2 * d]))
         for kk in range(2):
             for d in range(2):
-                k = kk + 2 - 2 * d
+                k = through[1 - d][kk]
                 m.send(nv.at[g, piece(quad[k][0], xs[1 + 2 * d], quad[k][1])], rb.at[g, d, k], R2[g][d][k], at(x=xs[1 + 2 * d]))
 
     def n_second(g):
         for kk in range(2):
             for d in range(2):
-                k = kk + 2 * d
+                k = through[d][kk]
                 m.wait(R1[g][d][kk])
                 rows = nv.at[g, piece(quad[k][0], xs[1 + 2 * d], quad[k][1])]
                 rows[...] += fw[g, d, kk]
@@ -389,7 +418,7 @@
             m.wait(R4[g][k])
         put[g].wait()
 
-    D1, D2, D3, D5, D6 = slots(2, 2, 4), slots(2, 2, 4), slots(2, 3), slots(2), slots(2)
+    D1, D2, D3, D5, D6 = slots(2, 2, 4), slots(2, CHUNKS, 2, 4), slots(2, CHUNKS, 3), slots(2, CHUNKS), slots(2, CHUNKS)
     root_put = pltpu.make_async_copy(fv.at[0, piece(zl, x, c)], extra.at[0], ls.at[5])
 
     def f_first(g):
@@ -397,48 +426,65 @@
             for kd in range(2):
                 m.send(fv.at[g, piece(kind[kd], units[j], 1 - c)], db.at[g, kd, j], D1[g][kd][j], at(c=1 - c))
 
-    def f_second(g):
-        for j in (2, 1, 3, 0):
+    def f_second(g, h):
+        part = pl.ds(h * PART, PART)
+        near_j = 1 if h == 0 else 3
+        for j in (2, 4 - near_j, near_j, 0):
             for kd in (1, 0):
-                rows = fv.at[g, piece(kind[kd], units[j], c)]
-                m.wait(D1[g][kd][j])
-                rows[...] += db[g, kd, j]
-                if j:
-                    m.send(rows, yb.at[g, kd, j], D2[g][kd][j], at(y=ys[j]))
-
-    def f_third(g):
+                rows = fv.at[g, chunk(kind[kd], units[j], c, h)]
+                if h == 0:
+                    m.wait(D1[g][kd][j])
+                rows[...] += db[g, kd, j, part]
+                if j == 2:
+                    m.send(rows, yb.at[g, kd, 2, part], D2[g][h][kd][2], at(y=ys[near_j]))
+                if j == 4 - near_j:
+                    m.send(rows, yb.at[g, kd, j, part], D2[g][h][kd][j], at(y=ys[j]))
+
+    def f_pass(g, h):
+        part = pl.ds(h * PART, PART)
+        near_j = 1 if h == 0 else 3
         for kd in (1, 0):
-            rows = fv.at[g, piece(kind[kd], units[0], c)]
-            for j in (1, 3, 2):
-                m.wait(D2[g][kd][j])
-            rows[...] += (yb[g, kd, 1] + yb[g, kd, 2]) + yb[g, kd, 3]
+            rows = fv.at[g, chunk(kind[kd], units[near_j], c, h)]
+            m.wait(D2[g][h][kd][2], PART)
+            rows[...] += yb[g, kd, 2, part]
+            m.send(rows, yb.at[g, kd, near_j, part], D2[g][h][kd][near_j], at(y=ys[near_j]))
+
+    def f_third(g, h):
+        part = pl.ds(h * PART, PART)
+        for kd in (1, 0):
+            rows = fv.at[g, chunk(kind[kd], units[0], c, h)]
+            for j in (1, 3):
+                m.wait(D2[g][h][kd][j], PART)
+            rows[...] += yb[g, kd, 1, part] + yb[g, kd, 3, part]
             if kd:
-                m.send(rows, zb.at[g, 0], D3[g][0], at(zl=1 - zl), home[g])
-                m.send(rows, zb.at[g, 1], D3[g][1], opposite, away[g])
+                m.send(rows, zb.at[g, 0, part], D3[g][h][0], at(zl=1 - zl), home[g])
+                m.send(rows, zb.at[g, 1, part], D3[g][h][1], opposite, away[g])
             else:
-                m.send(rows, zb.at[g, 2], D3[g][2], cross, away[g])
-
-    def f_fourth(g):
-        rows = fv.at[g, piece(prim, units[0], c)]
+                m.send(rows, zb.at[g, 2, part], D3[g][h][2], cross, away[g])
+
+    def f_fourth(g, h):
+        part = pl.ds(h * PART, PART)
+        rows = fv.at[g, chunk(prim, units[0], c, h)]
 
         def go():
             for e in range(3):
-                m.wait(D3[g][e])
-            rows[...] += (zb[g, 0] + zb[g, 1]) + zb[g, 2]
+                m.wait(D3[g][h][e], PART)
+            rows[...] += (zb[g, 0, part] + zb[g, 1, part]) + zb[g, 2, part]
 
         pl.when(home[g])(go)
-        if g == 0:
+        if g == 0 and h == CHUNKS - 1:
             guarded(at_home_0, root_put.start)
-        m.send(rows, hb.at[1, g], D5[g], at(x=units[0]), arrives[g])
+        m.send(rows, hb.at[1, g, h], D5[g][h], at(x=units[0]), arrives[g])
         if g == 1:
-            m.send(rows, extra.at[g], D6[g], source, stays)
-
-    def f_fifth(g):
-        guarded(passes[g], lambda: m.wait(D5[g]))
-        m.send(hb.at[1, g], extra.at[g], D6[g], passed_from[g], passes[g])
+            m.send(rows, extra.at[g, part], D6[g][h], source, stays)
+
+    def f_fifth(g, h):
+        guarded(passes[g], lambda: m.wait(D5[g][h], PART))
+        m.send(hb.at[1, g, h], extra.at[g, pl.ds(h * PART, PART)], D6[g][h], passed_from[g], passes[g])
 
     def f_finish(g):
-        guarded(gives_away[g], lambda: m.wait(D6[g]))
+        for h in range(CHUNKS):
+            guarded(gives_away[g], lambda: m.wait(D6[g][h], PART))
         if g == 0:
             guarded(at_home_0, root_put.wait)
 
@@ -450,18 +496,26 @@
     build_kernel(k_ref)
     for k in range(1, 4):
         i_spread(0, k)
-    j_relay(0)
-    j_relay(1)
-    j_entry(0)
+    j_relay(0, 0)
+    j_relay(0, 1)
+    j_entry(0, 0)
+    j_relay(1, 0)
+    j_entry(0, 1)
+    j_relay(1, 1)
     i_spread(1, 0)
-    j_entry(1)
-    j_other(0)
+    j_other(0, 0)
+    j_entry(1, 0)
+    j_other(0, 1)
+    j_entry(1, 1)
     i_forward(0)
-    j_other(1)
     for k in range(1, 4):
         i_spread(1, k)
+    j_pass(0)
+    j_other(1, 0)
+    j_other(1, 1)
     j_rows(0)
     i_finish(0)
+    j_pass(1)
     j_finish(0)
 
     def do(*steps):
@@ -472,14 +526,12 @@
         return run
 
     plan = {
-        (0, 1): do(lambda: j_rows(1)),
-        (0, 2): do(lambda: i_forward(1)),
+        (0, 1): do(lambda: i_forward(1)),
+        (0, 2): do(lambda: j_rows(1)),
         (1, 0): do(lambda: j_finish(1)),
         (2, 0): do(lambda: n_first(0), lambda: i_finish(1)),
-        (2, 2): do(lambda: n_second(0)),
-        (3, 0): do(lambda: f_first(1)),
-        (3, 1): do(lambda: f_second(1)),
-        (3, 2): do(lambda: n_third(0)),
+        (3, 0): do(lambda: f_first(1), lambda: n_second(0)),
+        (3, 2): do(lambda: f_second(1, 0), lambda: f_second(1, 1)),
     }
 
     def point(t, stage):
@@ -490,15 +542,27 @@
     transform_pairs(iv, jv, nv, fv, a, k_ref, wz_ref, wi_ref, ty_ref, tyi_ref, tx_ref, point)
     n_first(1)
     f_first(0)
-    f_second(0)
-    f_third(1)
+    f_pass(1, 0)
+    f_pass(1, 1)
+    f_second(0, 0)
+    f_second(0, 1)
+    f_third(1, 0)
+    f_third(1, 1)
+    n_third(0)
     n_second(1)
-    f_fourth(1)
-    f_third(0)
-    f_fifth(1)
-    f_fourth(0)
+    f_pass(0, 0)
+    f_pass(0, 1)
+    f_fourth(1, 0)
+    f_fourth(1, 1)
+    f_third(0, 0)
+    f_third(0, 1)
+    f_fifth(1, 0)
+    f_fifth(1, 1)
+    f_fourth(0, 0)
+    f_fourth(0, 1)
+    f_fifth(0, 0)
+    f_fifth(0, 1)
     n_third(1)
-    f_fifth(0)
     for g in range(2):
         n_finish(g)
         f_finish(g)
@@ -541,7 +605,7 @@
         out_shape=jax.ShapeDtypeStruct((6, 8, 9216), f32),
         in_specs=[an] + [vm] * 5,
         out_specs=an,
-        scratch_shapes=[pltpu.VMEM((N * N, 128), f32), pltpu.VMEM((6, 8, 9216), f32), pltpu.VMEM((8 * PIECE, 128), f32), pltpu.VMEM((8 * PIECE, 128), f32), pieces(2), pieces(2, 2)]
+        scratch_shapes=[pltpu.VMEM((N * N, 128), f32), pltpu.VMEM((6, 8, 9216), f32), pltpu.VMEM((8 * PIECE, 128), f32), pltpu.VMEM((8 * PIECE, 128), f32), pieces(2), pltpu.VMEM((2, 2, CHUNKS, PART, 128), f32)]
         + [big] * 4
         + [pltpu.VMEM((96 * AS, 128), f32), pieces(2, 2, 2), pieces(2, 2, 4), pieces(2, 2, 4), pieces(2, 3), pieces(2, 2, 4)]
         + [pltpu.SemaphoreType.DMA((SENDS,)), pltpu.SemaphoreType.DMA((RECEIVES,)), pltpu.SemaphoreType.DMA((16,))],

time: 182 us -> 179 us (0.984)
  the two profiles are of different devices: /device:TPU:8 before, /device:TPU:21 now
where the time goes in v6:
time: 179 us
  Pallas kernels  176 us (98%)
  local copies, waits for them, and re-layouts  2.8 us (2%)
    pallas_call x1, Pallas kernels, local(): pl.pallas_call(exchange, out_shape=jax.ShapeDtypeStruct((6, 8, 9216), f32...  176 us

profile of v6, /device:TPU:21, one launch (start us, length us, event | category | flops | bytes accessed | tf_op | source)
XLA Modules:
  0.0 178.6 jit_solution(6145547122698298561)
XLA Ops:
  0.0 175.8 %shard_map.64 = f32[6,8,9216]{2,1,0:T(8,128)} custom-call(f32[6,8,9216]{2,1,0:T(8,128)} %bitcast.3, bf16[4,256,256]{2,1,0:T(8,128)(2,1)} %constant.10.clone.wz_ref, bf16[4,256,256]{2,1,0:T(8,128)(2,1)} %constant.11.clone.wi_ref, bf16[192,192]{1,0:T(8,128)(2,1)} %constant.12.clone.ty_ref, bf16[192,192]{1,0:T(8,128)(2,1)} %constant.13.clone.tyi_ref, ...), custom_call_target="tpu_custom_call" | custom-call | tf_op jit(solution)/shard_map/pallas_call | solution.py:603
  175.8 2.8 %copy.8 = f32[8,6,9216]{2,0,1:T(8,128)} copy(f32[8,6,9216]{2,0,1:T(8,128)} %bitcast.2) | data formatting | bytes 3538944

commit v7 on v6

--- a/solution.py
+++ b/solution.py
@@ -11,7 +11,7 @@
 OMEGA = 0.106
 CELL = 41.05
 bf = jnp.bfloat16
-XB, VB, AS = 24, 24, 97
+XB, VB, AS = 32, 32, 97
 
 def split_np(t):
     t = t.astype(np.float32)

time: 179 us -> 178 us (level)
  no operation moved by 1% of the time
where the time goes in v7:
time: 178 us
  Pallas kernels  175 us (98%)
  local copies, waits for them, and re-layouts  2.8 us (2%)
    pallas_call x1, Pallas kernels, local(): pl.pallas_call(exchange, out_shape=jax.ShapeDtypeStruct((6, 8, 9216), f32...  175 us

profile of v7, /device:TPU:21, one launch (start us, length us, event | category | flops | bytes accessed | tf_op | source)
XLA Modules:
  0.0 177.7 jit_solution(10112422047047973288)
XLA Ops:
  0.0 174.9 %shard_map.64 = f32[6,8,9216]{2,1,0:T(8,128)} custom-call(f32[6,8,9216]{2,1,0:T(8,128)} %bitcast.3, bf16[4,256,256]{2,1,0:T(8,128)(2,1)} %constant.10.clone.wz_ref, bf16[4,256,256]{2,1,0:T(8,128)(2,1)} %constant.11.clone.wi_ref, bf16[192,192]{1,0:T(8,128)(2,1)} %constant.12.clone.ty_ref, bf16[192,192]{1,0:T(8,128)(2,1)} %constant.13.clone.tyi_ref, ...), custom_call_target="tpu_custom_call" | custom-call | tf_op jit(solution)/shard_map/pallas_call | solution.py:603
  174.9 2.8 %copy.8 = f32[8,6,9216]{2,0,1:T(8,128)} copy(f32[8,6,9216]{2,0,1:T(8,128)} %bitcast.2) | data formatting | bytes 3538944

commit v8 on v7

--- a/solution.py
+++ b/solution.py
@@ -11,7 +11,7 @@
 OMEGA = 0.106
 CELL = 41.05
 bf = jnp.bfloat16
-XB, VB, AS = 32, 32, 97
+XB, VB, AS = 32, 48, 97
 
 def split_np(t):
     t = t.astype(np.float32)

time: 178 us -> 177 us (level)
  no operation moved by 1% of the time
where the time goes in v8:
time: 177 us
  Pallas kernels  174 us (98%)
  local copies, waits for them, and re-layouts  2.8 us (2%)
    pallas_call x1, Pallas kernels, local(): pl.pallas_call(exchange, out_shape=jax.ShapeDtypeStruct((6, 8, 9216), f32...  174 us

profile of v8, /device:TPU:21, one launch (start us, length us, event | category | flops | bytes accessed | tf_op | source)
XLA Modules:
  0.0 177.2 jit_solution(13216696509049058687)
XLA Ops:
  0.0 174.4 %shard_map.64 = f32[6,8,9216]{2,1,0:T(8,128)} custom-call(f32[6,8,9216]{2,1,0:T(8,128)} %bitcast.3, bf16[4,256,256]{2,1,0:T(8,128)(2,1)} %constant.10.clone.wz_ref, bf16[4,256,256]{2,1,0:T(8,128)(2,1)} %constant.11.clone.wi_ref, bf16[192,192]{1,0:T(8,128)(2,1)} %constant.12.clone.ty_ref, bf16[192,192]{1,0:T(8,128)(2,1)} %constant.13.clone.tyi_ref, ...), custom_call_target="tpu_custom_call" | custom-call | tf_op jit(solution)/shard_map/pallas_call | solution.py:603
  174.4 2.8 %copy.8 = f32[8,6,9216]{2,0,1:T(8,128)} copy(f32[8,6,9216]{2,0,1:T(8,128)} %bitcast.2) | data formatting | bytes 3538944
